TPU v7x, 32 devices: a whole 2x2x4 slice. The times are simulated.
32 devices in a mesh: shape: 4 (over z), grp: 8 (over y, x, core).
Axes of the slice: x: 2, y: 2, z: 4, core: 2. Of those that a mesh axis runs over, the one named last changes fastest.
Arguments:
- latents: bfloat16 [128, 64, 64, 128], P(('shape', 'grp')), parts along dimension 0, may hold values from -6 to 6
- up_weight: bfloat16 [3, 3, 3, 128, 64], replicated, may hold values from -0.25 to 0.25
- first_weight: bfloat16 [3, 3, 3, 64, 64], replicated, may hold values from -0.15625 to 0.15625
- second_weight: bfloat16 [3, 3, 3, 64, 64], replicated, may hold values from -0.15625 to 0.15625
- brick_ids: int32 [512], P(('shape', 'grp')), parts along dimension 0, may hold values from -1 to 255, as said below
- brick_owner: int32 [512], P(('shape', 'grp')), parts along dimension 0, may hold values from -1 to 7, as said below
- neighbor_live: int32 [512, 27], P(('shape', 'grp')), parts along dimension 0, may hold values 0 or 1
Outputs:
- fine_bricks: bfloat16 [512, 32768], P(('shape', 'grp')), parts along dimension 0
There are 4 independent parts, one for each index of `shape`. A program takes and returns all parts, laid end to end along the dimension named above; an argument that names none is the same for every part. Nothing has to cross between parts.
Inputs may be any that keep to these rules, and one draw needn't show every extreme that they name: `brick_ids`: each device's block of 16 entries lists distinct bricks of its own panel by local number (x slowest, z fastest), -1 for an unused entry; every block uses 16 - 16 // 2 to 16 entries at any positions, and some block uses all of them. `brick_owner`: -1 exactly where brick_ids is -1. Within one device's block no owner appears more than 2 times among used entries, and one owner appears exactly 2 times among the used entries of every block.
All inputs are finite; a program needn't handle non-finite values. No bound on the sum of `neighbor_live` on one device may be relied on, other than what follows from the above.
Results may differ from a plain program's by a relative error of at most 0.0052.
Values may be sent and summed in bfloat16 or wider, within the bound.
No kernel may reach another device: no remote copies, remote signals or barrier semaphores. Data moves between devices by JAX's collectives and lax.ppermute only.
A program may use at most 128 MiB of HBM per device.

v0:
```python
import jax
import jax.numpy as jnp
from jax import lax
from jax.sharding import PartitionSpec as P

BE = 8
HB = 4
G = 64
PX = 4


parity_taps = (((1, 0),), ((2, 0), (0, 1)))


def extended_2(block, sides, width):
    for axis, dim in sides:
        count = lax.axis_size(axis)
        forward = [(i, i + 1) for i in range(count - 1)]
        backward = [(target, source) for source, target in forward]
        low = lax.ppermute(
            lax.slice_in_dim(block, block.shape[dim] - width, None, axis=dim), axis, forward
        )
        high = lax.ppermute(lax.slice_in_dim(block, 0, width, axis=dim), axis, backward)
        block = jnp.concatenate([low, block, high], axis=dim)
    return block


def upsample(regions, weight):
    sub_edge = regions.shape[1] - 1
    parity_grids = []
    for parity_x in range(2):
        plane_list = []
        for parity_y in range(2):
            line_list = []
            for parity_z in range(2):
                pieces = []
                kernels = []
                for tap_x, shift_x in parity_taps[parity_x]:
                    for tap_y, shift_y in parity_taps[parity_y]:
                        for tap_z, shift_z in parity_taps[parity_z]:
                            pieces.append(
                                regions[
                                    :,
                                    shift_x : shift_x + sub_edge,
                                    shift_y : shift_y + sub_edge,
                                    shift_z : shift_z + sub_edge,
                                    :,
                                ]
                            )
                            kernels.append(weight[tap_x, tap_y, tap_z])
                stacked = jnp.concatenate(pieces, axis=-1)
                kernel = jnp.concatenate(kernels, axis=0)
                line_list.append(
                    jnp.einsum(
                        "bxyzc,co->bxyzo", stacked, kernel, preferred_element_type=jnp.float32
                    )
                )
            plane_list.append(jnp.stack(line_list, axis=4))
        parity_grids.append(jnp.stack(plane_list, axis=3))
    alternated = jnp.stack(parity_grids, axis=2)
    return alternated.reshape(
        regions.shape[0], 2 * sub_edge, 2 * sub_edge, 2 * sub_edge, weight.shape[-1]
    )


def cell_mask(live_flags, full_edge):
    cell_pos = jnp.arange(full_edge, dtype=jnp.int32)
    neighbor_class = (cell_pos >= 2).astype(jnp.int32) + (cell_pos >= full_edge - 2).astype(
        jnp.int32
    )
    selector = (neighbor_class[:, None] == jnp.arange(3, dtype=jnp.int32)[None, :]).astype(
        jnp.float32
    )
    flag_cube = live_flags.reshape(live_flags.shape[0], 3, 3, 3)
    return jnp.einsum("bijk,xi,yj,zk->bxyz", flag_cube, selector, selector, selector)


def conv_valid(inputs, kernel):
    return lax.conv_general_dilated(
        inputs,
        kernel,
        (1, 1, 1),
        "VALID",
        dimension_numbers=("NDHWC", "DHWIO", "NDHWC"),
        preferred_element_type=jnp.float32,
    )


def refine(extended, full_mask, first_weight, second_weight):
    first_out = conv_valid(extended, first_weight)
    hidden = (jax.nn.silu(first_out) * full_mask[:, 1:-1, 1:-1, 1:-1, None]).astype(jnp.bfloat16)
    second_out = conv_valid(hidden, second_weight)
    refined = extended[:, 2:-2, 2:-2, 2:-2, :].astype(jnp.float32) + second_out
    return refined.astype(jnp.bfloat16).reshape(extended.shape[0], -1)


def neighbor_flags(brick_x, brick_y, brick_z, in_use, neighbor_live, bricks_long, bricks_across):
    offsets = jnp.arange(27, dtype=jnp.int32)
    step_x = offsets // 9 - 1
    step_y = offsets // 3 % 3 - 1
    step_z = offsets % 3 - 1
    near_x = brick_x[:, None] + step_x[None, :]
    near_y = brick_y[:, None] + step_y[None, :]
    near_z = brick_z[:, None] + step_z[None, :]
    inside = (
        (near_x >= 0)
        & (near_x < bricks_long)
        & (near_y >= 0)
        & (near_y < bricks_across)
        & (near_z >= 0)
        & (near_z < bricks_across)
    )
    chosen = (neighbor_live > 0) | (offsets == 13)[None, :]
    return (inside & chosen & in_use[:, None]).astype(jnp.float32)


def local(latents, up_weight, first_weight, second_weight, brick_ids, brick_owner, neighbor_live):
    group_size = lax.axis_size("grp")
    device_pos = lax.axis_index("grp")
    listed = brick_ids.shape[0]
    capacity = max(2, listed // group_size)
    slot_count = group_size * capacity
    across = G // HB
    panel_bricks = PX // HB
    channels = latents.shape[3]
    full_edge = BE + 4
    in_use = brick_ids >= 0
    safe_ids = jnp.maximum(brick_ids, 0)
    local_x = safe_ids // (across * across)
    brick_y = safe_ids // across % across
    brick_z = safe_ids % across
    rimmed = extended_2(latents, (("grp", 0),), 2)
    padded = jnp.pad(rimmed, ((0, 0), (1, 2), (1, 2), (0, 0)))

    def slice_region(start_x, start_y, start_z):
        starts = (start_x * HB + 1, start_y * HB, start_z * HB, jnp.int32(0))
        return lax.dynamic_slice(padded, starts, (HB + 3, HB + 3, HB + 3, channels))

    regions = jax.vmap(slice_region)(local_x, brick_y, brick_z)
    brick_x = device_pos * panel_bricks + local_x
    live_flags = neighbor_flags(
        brick_x, brick_y, brick_z, in_use, neighbor_live, panel_bricks * group_size, across
    )
    full_mask = cell_mask(live_flags, full_edge)
    extended = (upsample(regions, up_weight) * full_mask[..., None]).astype(jnp.bfloat16)
    owner_onehot = (
        (brick_owner[:, None] == jnp.arange(group_size, dtype=jnp.int32)[None, :]) & in_use[:, None]
    ).astype(jnp.int32)
    earlier = jnp.cumsum(owner_onehot, axis=0) - owner_onehot
    owner_rank = jnp.sum(earlier * owner_onehot, axis=1)
    target = jnp.where(in_use, brick_owner * capacity + owner_rank, slot_count)
    refined = refine(extended, full_mask, first_weight, second_weight)
    out_rows = (
        jnp.zeros((slot_count, refined.shape[1]), jnp.bfloat16).at[target].set(refined, mode="drop")
    )
    return lax.all_to_all(out_rows, "grp", split_axis=0, concat_axis=0, tiled=True)


def solution(mesh):
    in_specs = (
        P(("shape", "grp"), None, None, None),
        P(),
        P(),
        P(),
        P(("shape", "grp")),
        P(("shape", "grp")),
        P(("shape", "grp"), None),
    )
    out_specs = P(("shape", "grp"), None)
    return jax.shard_map(local, mesh=mesh, in_specs=in_specs, out_specs=out_specs, check_vma=False)
```

profile of v0, /device:TPU:0, one launch (start us, length us, event | category | flops | bytes accessed | tf_op | source)
XLA Modules:
  0.0 392.2 jit_solution(6102248316999089592)
XLA Ops:
  0.0 5.2 %fusion.103 = (bf16[2,64,64,128]{3,2,1,0:T(8,128)(2,1)}, bf16[2,64,64,128]{3,2,1,0:T(8,128)(2,1)}) fusion(bf16[4,64,64,128]{3,2,1,0:T(8,128)(2,1)} %param.7), kind=kLoop, calls=%fused_computation.196 | loop fusion | bytes 8388608 | tf_op jit(solution)/shard_map/slice | solution.py:21
  5.2 3.9 collective-permute-start
  9.1 1.3 collective-permute-start.1
  12.0 0.9 copy.28
  13.0 1.2 slice.203
  14.2 2.7 copy.29
  17.0 12.4 %select_maximum_fusion = bf16[8,67,67,128]{3,2,1,0:T(8,128)(2,1)} fusion(bf16[2,64,64,128]{3,2,1,0:T(8,128)(2,1)} %collective-permute-done.1, bf16[4,64,64,128]{3,2,1,0:T(8,128)(2,1)} %param.7, bf16[2,64,64,128]{3,2,1,0:T(8,128)(2,1)} %collective-permute-done), kind=kLoop, calls=%fused_computation.12 | loop fusion | flops 87337984 | bytes 17582080 | tf_op jit(solution)/shard_map/concatenate | solution.py:24
  29.4 66.3 %while.1 = (s32[]{:T(128)}, bf16[8,67,67,128]{3,2,1,0:T(8,128)(2,1)}, s32[16,4]{0,1:T(4,128)S(1)}, bf16[16,7,7,7,128]{4,3,2,1,0:T(8,128)(2,1)}, s32[]{:T(128)}) while((s32[]{:T(128)}, bf16[8,67,67,128]{3,2,1,0:T(8,128)(2,1)}, s32[16,4]{0,1:T(4,128)S(1)}, bf16[16,7,7,7,128]{4,3,2,1,0:T(8,128)(2,1)}, s32[]{:T(128)}) %tuple.56), condition=%wide.while_cond, body=%wide.while_body.sunk | while | flops 2 | bytes 202873 | solution.py:137
  29.5 0.5 fusion.112
  30.0 3.5 bitcast_dynamic-update-slice_fusion.2
  33.6 0.5 fusion.112
  34.2 3.5 bitcast_dynamic-update-slice_fusion.2
  37.8 0.5 fusion.112
  38.3 3.5 bitcast_dynamic-update-slice_fusion.2
  41.9 0.5 fusion.112
  42.5 3.5 bitcast_dynamic-update-slice_fusion.2
  46.0 0.5 fusion.112
  46.6 3.5 bitcast_dynamic-update-slice_fusion.2
  50.2 0.5 fusion.112
  50.7 3.5 bitcast_dynamic-update-slice_fusion.2
  54.3 0.5 fusion.112
  54.9 3.5 bitcast_dynamic-update-slice_fusion.2
  58.5 0.5 fusion.112
  59.0 3.5 bitcast_dynamic-update-slice_fusion.2
  62.6 0.5 fusion.112
  63.1 3.5 bitcast_dynamic-update-slice_fusion.2
  66.8 0.5 fusion.112
  67.3 3.5 bitcast_dynamic-update-slice_fusion.2
  70.9 0.5 fusion.112
  71.5 3.5 bitcast_dynamic-update-slice_fusion.2
  75.1 0.5 fusion.112
  75.6 3.5 bitcast_dynamic-update-slice_fusion.2
  79.2 0.5 fusion.112
  79.7 3.5 bitcast_dynamic-update-slice_fusion.2
  83.3 0.5 fusion.112
  83.9 3.5 bitcast_dynamic-update-slice_fusion.2
  87.5 0.5 fusion.112
  88.0 3.5 bitcast_dynamic-update-slice_fusion.2
  91.6 0.5 fusion.112
  92.2 3.5 bitcast_dynamic-update-slice_fusion.2
  95.7 1.6 copy.18
  97.3 2.4 fusion.104
  103.1 0.6 fusion.28
  103.7 0.6 fusion.29
  104.3 1.1 fusion.30
  105.4 1.1 maximum_bitcast_fusion.2
  106.5 3.9 maximum_bitcast_fusion
  110.4 2.0 convolution_bitcast_fusion.1
  112.4 0.6 fusion.27
  113.0 1.1 fusion.33
  114.2 1.1 fusion.36
  115.3 1.0 maximum_bitcast_fusion.4
  116.3 3.7 maximum_bitcast_fusion.1
  119.9 12.9 %pad_maximum_fusion = f32[16,6,2,6,2,6,2,64]{7,0,5,3,1,6,4,2:T(8,128)} fusion(f32[16,6,1,6,2,6,2,64]{7,0,5,3,1,6,4,2:T(8,128)} %maximum_bitcast_fusion.1, f32[16,6,1,6,2,6,2,64]{7,0,5,3,1,6,4,2:T(8,128)} %maximum_bitcast_fusion), kind=kLoop, calls=%fused_computation.10 | loop fusion | flops 1769472 | bytes 14155776 | tf_op jit(solution)/shard_map/stack | solution.py:60
  132.9 12.1 %copy.26 = f32[16,6,2,6,2,6,2,64]{7,0,6,5,4,3,2,1:T(8,128)} copy(f32[16,6,2,6,2,6,2,64]{7,0,5,3,1,6,4,2:T(8,128)} %pad_maximum_fusion) | data formatting | bytes 14155776 | tf_op jit(solution)/shard_map/stack | solution.py:60
  144.9 8.2 %multiply_convert_fusion = bf16[16,12,12,12,64]{4,0,3,2,1:T(8,128)(2,1)S(1)} fusion(f32[16,12,12,12,64]{4,0,3,2,1:T(8,128)} %bitcast.161, f32[16,12,12,12]{0,3,2,1:T(8,128)S(1)} %copy.28), kind=kLoop, calls=%fused_computation.11 | loop fusion | flops 3538944 | bytes 10727424 | tf_op jit(solution)/shard_map/convert_element_type | solution.py:145
  153.2 163.8 %fusion.105 = f32[16,10,10,10,64]{4,0,3,2,1:T(8,128)S(1)} fusion(bf16[16,12,12,12,64]{4,0,3,2,1:T(8,128)(2,1)S(1)} %multiply_convert_fusion, bf16[3,3,3,64,64]{4,3,2,1,0:T(8,128)(2,1)S(1)} %copy-done), kind=kOutput, calls=%fused_computation.198 | convolution fusion | flops 3538944000 | bytes 7856128 | tf_op jit(solution)/shard_map/conv_general_dilated | solution.py:79
  316.9 9.2 %add_convert_fusion = bf16[16,8,8,8,64]{4,0,3,2,1:T(8,128)(2,1)S(1)} fusion(bf16[16,12,12,12,64]{4,0,3,2,1:T(8,128)(2,1)S(1)} %multiply_convert_fusion, bf16[3,3,3,64,64]{4,3,2,1,0:T(8,128)(2,1)S(1)} %copy-done.9, f32[16,10,10,10,64]{4,0,3,2,1:T(8,128)S(1)} %fusion.105, f32[16,10,10,10]{0,3,2,1:T(8,128)S(1)} %copy-done.4), kind=kOutput, calls=%fused_computation.24 | convolution fusion | flops 1819656192 | bytes 6478336 | tf_op jit(solution)/shard_map/conv_general_dilated | solution.py:79
  326.1 0.6 copy.30
  326.7 2.5 reshape.104
  329.2 2.9 scatter_custom_fusion
  332.1 0.7 all_to_all.8
  332.8 58.1 %all_to_all.12 = bf16[8,2,32768]{2,1,0:T(2,128)(2,1)S(1)} all-to-all(bf16[8,2,32768]{2,1,0:T(2,128)(2,1)S(1)} %all_to_all.8), channel_id=1, replica_groups=mesh['shape'=4,'grp'=8] {'grp'}, dimensions={0} | all-to-all | bytes 2097152 | tf_op jit(solution)/shard_map/all_to_all | solution.py:156
  391.0 1.2 all_to_all.10
  (74 shorter events, 6.3 us)
Async XLA Ops:
  0.0 153.1 %copy-start = (bf16[3,3,3,64,64]{4,3,2,1,0:T(8,128)(2,1)S(1)}, bf16[3,3,3,64,64]{4,3,2,1,0:T(8,128)(2,1)}, u32[]{:S(2)}) copy-start(bf16[3,3,3,64,64]{4,3,2,1,0:T(8,128)(2,1)} %param.9) | copy-start | bytes 663556
  0.0 10.4 %copy-start.8 = (s32[16]{0:T(128)S(1)}, s32[16]{0:T(128)}, u32[]{:S(2)}) copy-start(s32[16]{0:T(128)} %param.11) | copy-start | bytes 196
  0.0 10.5 %copy-start.7 = (s32[16]{0:T(128)S(1)}, s32[16]{0:T(128)}, u32[]{:S(2)}) copy-start(s32[16]{0:T(128)} %param.12) | copy-start | bytes 196
  0.0 10.9 %copy-start.6 = (s32[16,27]{1,0:T(8,128)S(1)}, s32[16,27]{1,0:T(8,128)}, u32[]{:S(2)}) copy-start(s32[16,27]{1,0:T(8,128)} %param.13) | copy-start | bytes 5188
  5.2 11.7 %copy-start.5 = (bf16[3,3,3,128,64]{3,4,2,1,0:T(8,128)(2,1)S(1)}, bf16[3,3,3,128,64]{3,4,2,1,0:T(8,128)(2,1)}, u32[]{:S(2)}) copy-start(bf16[3,3,3,128,64]{3,4,2,1,0:T(8,128)(2,1)} %param.8) | copy-start | bytes 1327108
  5.2 11.8 %collective-permute-start = (bf16[2,64,64,128]{3,2,1,0:T(8,128)(2,1)}, bf16[2,64,64,128]{3,2,1,0:T(8,128)(2,1)}, u32[]{:S(2)}, u32[]{:S(2)}) collective-permute-start(bf16[2,64,64,128]{3,2,1,0:T(8,128)(2,1)} %get-tuple-element.30), channel_id=1, source_target_pairs={{0,1},{1,2},{2,3},{3,4},{4,5},{5,6},{6,7},{8,9},{9,10},{10,11},{11... | collective-permute-start | bytes 6291464 | tf_op jit(solution)/shard_map/ppermute | solution.py:20
  9.1 7.9 %collective-permute-start.1 = (bf16[2,64,64,128]{3,2,1,0:T(8,128)(2,1)}, bf16[2,64,64,128]{3,2,1,0:T(8,128)(2,1)}, u32[]{:S(2)}, u32[]{:S(2)}) collective-permute-start(bf16[2,64,64,128]{3,2,1,0:T(8,128)(2,1)} %get-tuple-element.31), channel_id=1, source_target_pairs={{1,0},{2,1},{3,2},{4,3},{5,4},{6,5},{7,6},{9,8},{10,9},{11,10},{12... | collective-permute-start | bytes 6291464 | tf_op jit(solution)/shard_map/ppermute | solution.py:23
  110.4 2.6 copy-start.3
  113.0 1.2 copy-start.2
  153.1 163.8 %copy-start.4 = (f32[16,10,10,10]{0,3,2,1:T(8,128)S(1)}, f32[16,10,10,10]{0,3,2,1:T(8,128)}, u32[]{:S(2)}) copy-start(f32[16,10,10,10]{0,3,2,1:T(8,128)} %copy.29) | copy-start | bytes 192004
  153.1 163.8 %copy-start.9 = (bf16[3,3,3,64,64]{4,3,2,1,0:T(8,128)(2,1)S(1)}, bf16[3,3,3,64,64]{4,3,2,1,0:T(8,128)(2,1)}, u32[]{:S(2)}) copy-start(bf16[3,3,3,64,64]{4,3,2,1,0:T(8,128)(2,1)} %param.10) | copy-start | bytes 663556
  326.7 65.5 %copy-start.1 = (bf16[3,3,3,64,64]{4,3,2,1,0:T(8,128)(2,1)S(1)}, bf16[3,3,3,64,64]{4,3,2,1,0:T(8,128)(2,1)}, u32[]{:S(2)}) copy-start(bf16[3,3,3,64,64]{4,3,2,1,0:T(8,128)(2,1)} %param.9) | copy-start | bytes 663556
where the time goes:
time: 394 us; the launch traced here: 392 us
  matrix products  181 us (46%)
  local copies, waits for them, and re-layouts  104 us (26%)
  blocking collectives  58.1 us (15%)
  other arithmetic  43.7 us (11%)
  starting transfers between devices  5.18 us (1%)
    conv_general_dilated x2, matrix products, conv_valid(): lax.conv_general_dilated(inputs, kernel, (1, 1, 1), 'VALID', dimension_nu...  173 us
    gather x48, local copies, waits for them, and re-layouts  66.2 us
    all_to_all x1, blocking collectives, local(): lax.all_to_all(out_rows, 'grp', split_axis=0, concat_axis=0, tiled=True)  58.1 us
    another operation x3, other arithmetic, upsample(): alternated = jnp.stack(parity_grids, axis=2)  20.5 us
    concatenate x1, other arithmetic, extended_2(): block = jnp.concatenate([low, block, high], axis=dim)  12.4 us
    another operation x1, local copies, waits for them, and re-layouts, upsample(): alternated = jnp.stack(parity_grids, axis=2)  12.1 us
    convert_element_type x1, other arithmetic, local(): (upsample(regions, up_weight) * full_mask[..., None]).astype(jnp.bfloat16)  8.17 us
  transfers between devices with their start and end apart: 2, of which 0 were waited for; matrix products, arithmetic and copies ran while one was open for 2% of the time, Pallas kernels for 0%

commit v1 on v0

v1 whole, which is shorter than its diff:
```python
import jax
import jax.numpy as jnp
from jax import lax
from jax.experimental import pallas as pl
from jax.experimental.pallas import tpu as pltpu
from jax.sharding import PartitionSpec as P

BE = 8
HB = 4
EDGE = HB + 3
WIN = 16

taps = (((1, 0),), ((2, 0), (0, 1)))


def slot_windows(slot_ids, grid):
    across = grid // HB
    slots = slot_ids.shape[0]
    safe = jnp.maximum(slot_ids, 0)
    low_y = safe // across % across * HB - 1
    low_z = safe % across * HB - 1
    start_y = jnp.clip(low_y, 0, grid - EDGE)
    start_z = jnp.clip(low_z // 8 * 8, 0, grid - WIN)
    starts = jnp.stack([start_y, low_y - start_y, start_z]).astype(jnp.int32)
    step = jnp.arange(EDGE, dtype=jnp.int32)
    place = jnp.arange(slots, dtype=jnp.int32)
    row = jnp.arange(WIN, dtype=jnp.int32)
    same = (place[:, None] == place[None, :]) & (slot_ids >= 0)[:, None]
    wanted = (low_z - start_z)[None, :] + step[:, None]
    hit = (
        same[None, None, :, :, None]
        & (row[None, None, None, None, :] == wanted[None, :, :, None, None])
    )
    inside = low_y + EDGE - 1 <= grid
    keep = jnp.stack([jnp.ones_like(inside), inside])
    hit = hit & keep[:, None, :, None, None]
    return starts, hit.astype(jnp.bfloat16).reshape(2, EDGE * slots, slots * WIN)


def gather(latents, jobs):
    grid = latents.shape[1]
    channels = latents.shape[3]
    slots = jobs[0][0].shape[0]
    prepared = [slot_windows(ids, grid) for ids, _, _ in jobs]
    starts = jnp.stack([one[0] for one in prepared])
    picks = jnp.stack([one[1] for one in prepared])

    def kernel(starts_ref, latents_ref, picks_ref, *refs):
        outs = refs[: len(jobs)]
        wins = refs[len(jobs) : 2 * len(jobs)]
        sems = refs[2 * len(jobs)]
        copies = []
        for job, (_, plane, count) in enumerate(jobs):
            for slot in range(slots):
                copy = pltpu.make_async_copy(
                    latents_ref.at[
                        pl.ds(plane, count),
                        pl.ds(starts_ref[job, 0, slot], EDGE),
                        pl.ds(pl.multiple_of(starts_ref[job, 2, slot], 8), WIN),
                        :,
                    ],
                    wins[job].at[slot],
                    sems.at[job, slot],
                )
                copy.start()
                copies.append(copy)
        for copy in copies:
            copy.wait()

        def line(y, carry):
            late = (y >= EDGE - 2).astype(jnp.int32)
            for job, (_, _, count) in enumerate(jobs):
                rows = []
                for slot in range(slots):
                    rows.append(jnp.clip(y + starts_ref[job, 1, slot], 0, EDGE - 1))
                planes = []
                for x in range(count):
                    planes.append(
                        jnp.concatenate(
                            [wins[job][slot, x, rows[slot]] for slot in range(slots)], axis=0
                        )
                    )
                block = jnp.concatenate(planes, axis=1)
                cut = jnp.dot(
                    picks_ref[job, late], block, preferred_element_type=jnp.float32
                ).astype(jnp.bfloat16)
                for x in range(count):
                    outs[job][x, y] = cut[:, x * channels : (x + 1) * channels].reshape(
                        EDGE, slots, channels
                    )
            return carry

        lax.fori_loop(0, EDGE, line, 0)

    vmem = pl.BlockSpec(memory_space=pltpu.VMEM)
    return pl.pallas_call(
        kernel,
        in_specs=[
            pl.BlockSpec(memory_space=pltpu.SMEM),
            pl.BlockSpec(memory_space=pl.ANY),
            vmem,
        ],
        out_specs=[vmem] * len(jobs),
        out_shape=[
            jax.ShapeDtypeStruct((count, EDGE, EDGE, slots, channels), jnp.bfloat16)
            for _, _, count in jobs
        ],
        scratch_shapes=[
            pltpu.VMEM((slots, count, EDGE, WIN, channels), jnp.bfloat16)
            for _, _, count in jobs
        ]
        + [pltpu.SemaphoreType.DMA((len(jobs), slots))],
        compiler_params=pltpu.CompilerParams(vmem_limit_bytes=48 << 20),
        cost_estimate=pl.CostEstimate(
            flops=100_000_000, bytes_accessed=4_000_000, transcendentals=0
        ),
    )(starts, latents, picks)


def paired_up(weight):
    depth, width = weight.shape[3:]
    zero = jnp.zeros((3, depth, width), weight.dtype)
    lookup = {(parity, shift): tap for parity in (0, 1) for tap, shift in taps[parity]}
    rows = []
    for dy in (0, 1):
        for dz in (0, 1):
            cols = []
            for py in (0, 1):
                for pz in (0, 1):
                    ty = lookup.get((py, dy))
                    tz = lookup.get((pz, dz))
                    cols.append(zero if ty is None or tz is None else weight[:, ty, tz])
            rows.append(jnp.concatenate(cols, axis=2))
    return jnp.concatenate(rows, axis=1)


def paired_conv(weight):
    depth, width = weight.shape[3:]
    zero = jnp.zeros((3, depth, width), weight.dtype)
    rows = []
    for dy in (0, 1):
        for dz in (0, 1):
            for iy in (0, 1):
                for iz in (0, 1):
                    cols = []
                    for oy in (0, 1):
                        for oz in (0, 1):
                            ky = 2 * dy + iy - oy
                            kz = 2 * dz + iz - oz
                            inside = 0 <= ky <= 2 and 0 <= kz <= 2
                            cols.append(weight[:, ky, kz] if inside else zero)
                    rows.append(jnp.concatenate(cols, axis=2))
    return jnp.concatenate(rows, axis=1).reshape(-1, 4 * width)


def decode(low, own, high, live, up_pairs, first_pairs, second_pairs):
    slots = own.shape[3]
    c1 = own.shape[4]
    quad = up_pairs.shape[2]
    c2 = quad // 4
    epairs = BE // 2 + 2
    hpairs = BE // 2 + 1
    opairs = BE // 2
    eedge = BE + 4
    hedge = BE + 2

    def kernel(low_ref, own_ref, high_ref, live_ref, up_ref, first_ref, second_ref, out_ref,
               reg, ext, hid, emask, hmask):
        reg[0] = low_ref[0]
        reg[1 : 1 + HB] = own_ref[...]
        reg[1 + HB : 3 + HB] = high_ref[...]
        flags = live_ref[...]
        wide = [
            jnp.broadcast_to(flags[:, n : n + 1], (slots, 2 * c2)).astype(jnp.float32)
            for n in range(27)
        ]
        left = lax.broadcasted_iota(jnp.int32, (slots, 2 * c2), 1) < c2

        def pair_class(p):
            return 0 if p == 0 else 2 if p == epairs - 1 else 1

        def cell_class(h):
            return 0 if h == 0 else 2 if h == hedge - 1 else 1

        for cx in range(3):
            for py in range(epairs):
                for pz in range(epairs):
                    n = cx * 9 + pair_class(py) * 3 + pair_class(pz)
                    emask[cx, py, pz] = wide[n].astype(jnp.bfloat16)
            for py in range(hpairs):
                for pz in range(hpairs):
                    for ty in (0, 1):
                        n = cx * 9 + cell_class(2 * py + ty) * 3
                        both = jnp.where(
                            left,
                            wide[n + cell_class(2 * pz)],
                            wide[n + cell_class(2 * pz + 1)],
                        )
                        hmask[cx, py, pz, :, ty * 2 * c2 : (ty + 1) * 2 * c2] = both.astype(
                            jnp.bfloat16
                        )

        def up(px, carry):
            def patch(x):
                return jnp.concatenate(
                    [
                        reg[x, dy : dy + epairs, dz : dz + epairs].reshape(-1, c1)
                        for dy in (0, 1)
                        for dz in (0, 1)
                    ],
                    axis=1,
                )

            cx = jnp.where(px == 0, 0, jnp.where(px == epairs - 1, 2, 1))
            mask = emask[cx].reshape(-1, 2 * c2)
            mask = jnp.concatenate([mask, mask], axis=1)
            first = patch(px)
            even = jnp.dot(first, up_ref[1], preferred_element_type=jnp.float32)
            ext[2 * px] = (even.astype(jnp.bfloat16) * mask).reshape(epairs, epairs, slots, quad)
            odd = jnp.dot(first, up_ref[2], preferred_element_type=jnp.float32)
            odd += jnp.dot(patch(px + 1), up_ref[0], preferred_element_type=jnp.float32)
            ext[2 * px + 1] = (odd.astype(jnp.bfloat16) * mask).reshape(
                epairs, epairs, slots, quad
            )
            return carry

        lax.fori_loop(0, epairs, up, 0)

        def conv(source, x, pairs, weight_ref):
            pieces = [
                source[x + kx, dy : dy + pairs, dz : dz + pairs].reshape(-1, quad)
                for kx in range(3)
                for dy in (0, 1)
                for dz in (0, 1)
            ]
            return jnp.dot(
                jnp.concatenate(pieces, axis=1),
                weight_ref[...],
                preferred_element_type=jnp.float32,
            )

        def first(x, carry):
            value = conv(ext, x, hpairs, first_ref)
            cx = jnp.where(x == 0, 0, jnp.where(x == hedge - 1, 2, 1))
            value = (value * (1.0 / (1.0 + jnp.exp(-value)))).astype(jnp.bfloat16)
            value = value * hmask[cx].reshape(-1, quad)
            hid[x] = value.reshape(hpairs, hpairs, slots, quad)
            return carry

        lax.fori_loop(0, hedge, first, 0)

        def second(x, carry):
            value = conv(hid, x, opairs, second_ref)
            centre = ext[x + 2, 1 : 1 + opairs, 1 : 1 + opairs].reshape(-1, quad)
            value = (value + centre.astype(jnp.float32)).astype(jnp.bfloat16)
            value = value.reshape(opairs, opairs, slots, quad)
            base = pl.multiple_of(x * (BE * BE * c2), 128)
            for py in range(opairs):
                for ty in (0, 1):
                    line = jnp.concatenate(
                        [
                            value[py, pz, :, ty * 2 * c2 : (ty + 1) * 2 * c2]
                            for pz in range(opairs)
                        ],
                        axis=1,
                    )
                    shift = (2 * py + ty) * BE * c2
                    out_ref[:, pl.ds(pl.multiple_of(base + shift, 128), BE * c2)] = line
            return carry

        lax.fori_loop(0, BE, second, 0)

    vmem = pl.BlockSpec(memory_space=pltpu.VMEM)
    return pl.pallas_call(
        kernel,
        in_specs=[vmem] * 7,
        out_specs=vmem,
        out_shape=jax.ShapeDtypeStruct((slots, BE * BE * BE * c2), jnp.bfloat16),
        scratch_shapes=[
            pltpu.VMEM((EDGE, EDGE, EDGE, slots, c1), jnp.bfloat16),
            pltpu.VMEM((eedge, epairs, epairs, slots, quad), jnp.bfloat16),
            pltpu.VMEM((hedge, hpairs, hpairs, slots, quad), jnp.bfloat16),
            pltpu.VMEM((3, epairs, epairs, slots, 2 * c2), jnp.bfloat16),
            pltpu.VMEM((3, hpairs, hpairs, slots, quad), jnp.bfloat16),
        ],
        compiler_params=pltpu.CompilerParams(vmem_limit_bytes=56 << 20),
        cost_estimate=pl.CostEstimate(
            flops=12_000_000_000, bytes_accessed=8_000_000, transcendentals=1_000_000
        ),
    )(low, own, high, live, up_pairs, first_pairs, second_pairs)


def neighbor_flags(brick_x, brick_y, brick_z, in_use, neighbor_live, bricks_long, bricks_across):
    offsets = jnp.arange(27, dtype=jnp.int32)
    step_x = offsets // 9 - 1
    step_y = offsets // 3 % 3 - 1
    step_z = offsets % 3 - 1
    near_x = brick_x + step_x[None, :]
    near_y = brick_y[:, None] + step_y[None, :]
    near_z = brick_z[:, None] + step_z[None, :]
    inside = (
        (near_x >= 0)
        & (near_x < bricks_long)
        & (near_y >= 0)
        & (near_y < bricks_across)
        & (near_z >= 0)
        & (near_z < bricks_across)
    )
    chosen = (neighbor_live > 0) | (offsets == 13)[None, :]
    return (inside & chosen & in_use[:, None]).astype(jnp.int32)


def exchange(windows, group, shift):
    lead = windows.shape[:3]
    slots, channels = windows.shape[3:]
    split = windows.reshape(-1, group, slots // group, channels)
    moved = lax.all_to_all(split, "grp", split_axis=1, concat_axis=1, tiled=True)
    if shift:
        moved = jnp.roll(moved, shift, axis=1)
    return moved.reshape(*lead, slots, channels)


def local(latents, up_weight, first_weight, second_weight, brick_ids, brick_owner, neighbor_live):
    group = lax.axis_size("grp")
    me = lax.axis_index("grp")
    listed = brick_ids.shape[0]
    capacity = max(2, listed // group)
    slots = group * capacity
    grid = latents.shape[1]
    across = grid // HB
    assert latents.shape[0] == HB

    in_use = brick_ids >= 0
    safe_ids = jnp.maximum(brick_ids, 0)
    entry = jnp.arange(listed, dtype=jnp.int32)
    before = (
        (brick_owner[:, None] == brick_owner[None, :])
        & in_use[None, :]
        & (entry[None, :] < entry[:, None])
    )
    rank = jnp.sum(before.astype(jnp.int32), axis=1)
    target = jnp.where(in_use, brick_owner * capacity + rank, slots)
    chosen = (target[None, :] == jnp.arange(slots, dtype=jnp.int32)[:, None]).astype(jnp.int32)
    slot_ids = jnp.sum(chosen * (brick_ids[None, :] + 1), axis=1) - 1
    flags = neighbor_flags(
        me, safe_ids // across % across, safe_ids % across, in_use, neighbor_live, group, across
    )
    slot_flags = jnp.sum(chosen[:, :, None] * flags[None, :, :], axis=1)

    message = jnp.concatenate(
        [jnp.broadcast_to(slot_ids, (group, slots)), slot_flags.reshape(group, capacity * 27)],
        axis=1,
    )
    heard = lax.all_to_all(message, "grp", split_axis=0, concat_axis=0, tiled=True)
    live = heard[:, slots:].reshape(slots, 27)
    ids_of = heard[:, :slots]
    below = lax.dynamic_index_in_dim(ids_of, (me + group - 1) % group, 0, keepdims=False)
    above = lax.dynamic_index_in_dim(ids_of, (me + 1) % group, 0, keepdims=False)
    below = jnp.where(me > 0, below, -1)
    above = jnp.where(me < group - 1, above, -1)

    (own,) = gather(latents, [(slot_ids, 0, HB)])
    high, low = gather(latents, [(below, 0, 2), (above, HB - 1, 1)])
    own = exchange(own, group, 0)
    high = exchange(high, group, -1)
    low = exchange(low, group, 1)
    return decode(
        low, own, high, live,
        paired_up(up_weight), paired_conv(first_weight), paired_conv(second_weight),
    )


def solution(mesh):
    in_specs = (
        P(("shape", "grp"), None, None, None),
        P(),
        P(),
        P(),
        P(("shape", "grp")),
        P(("shape", "grp")),
        P(("shape", "grp"), None),
    )
    out_specs = P(("shape", "grp"), None)
    return jax.shard_map(local, mesh=mesh, in_specs=in_specs, out_specs=out_specs, check_vma=False)
```

time: 394 us -> 87.1 us (0.22)
  matrix products: 181 us -> 0 us
  local copies, waits for them, and re-layouts: 104 us -> 19.2 us
  blocking collectives: 58.1 us -> 0 us
  other arithmetic: 43.7 us -> 11.8 us
  Pallas kernels: 0 us -> 25.8 us
  waiting for transfers between devices: 0.01 us -> 12.4 us
  starting transfers between devices: 5.18 us -> 16.6 us
    conv_general_dilated x2 -> x0, matrix products: 173 us -> none  [conv_valid(): lax.conv_general_dilated(inputs, kernel, (1, 1, 1), 'VALID', dimension_nu...]
    gather x49 -> x0, local copies, waits for them, and re-layouts: 67.9 us -> none
    all_to_all x1 -> x0, blocking collectives: 58.1 us -> none  [local(): lax.all_to_all(out_rows, 'grp', split_axis=0, concat_axis=0, tiled=True)]
    pallas_call x0 -> x3, Pallas kernels: none -> 25.8 us  [the longest x1 20.5 us: decode(): pl.pallas_call(kernel, in_specs=[vmem] * 7, out_specs=vmem, out_shape=jax...]
    another operation x6 -> x5, other arithmetic: 22.6 us -> 0.72 us  [the longest x4 0.7 us: gather(): starts = jnp.stack([one[0] for one in prepared])]
    all_to_all x0 -> x4, starting transfers between devices: none -> 16.6 us  [the longest x3 11.4 us: exchange(): lax.all_to_all(split, 'grp', split_axis=1, concat_axis=1, tiled=True)]
    all_to_all x0 -> x4, waiting for transfers between devices: none -> 12.4 us  [the longest x3 12.4 us: exchange(): lax.all_to_all(split, 'grp', split_axis=1, concat_axis=1, tiled=True)]
    another operation x1 -> x5, local copies, waits for them, and re-layouts: 12.1 us -> 0.71 us  [the longest x3 0.69 us: slot_windows(): keep = jnp.stack([jnp.ones_like(inside), inside])]
  transfers between devices with their start and end apart: 2 -> 4, of which waited for: 0 -> 3; matrix products, arithmetic and copies ran while one was open for 2% -> 20% of each run, Pallas kernels for 0% -> 3%
where the time goes in v1:
time: 87.1 us; the launch traced here: 86.4 us
  Pallas kernels  25.8 us (30%)
  local copies, waits for them, and re-layouts  19.2 us (22%)
  starting transfers between devices  16.6 us (19%)
  waiting for transfers between devices  12.4 us (14%)
  other arithmetic  11.8 us (14%)
    pallas_call x1, Pallas kernels, decode(): pl.pallas_call(kernel, in_specs=[vmem] * 7, out_specs=vmem, out_shape=jax...  20.5 us
    all_to_all x3, waiting for transfers between devices, exchange(): lax.all_to_all(split, 'grp', split_axis=1, concat_axis=1, tiled=True)  12.4 us
    all_to_all x3, starting transfers between devices, exchange(): lax.all_to_all(split, 'grp', split_axis=1, concat_axis=1, tiled=True)  11.4 us
    unnamed x20, local copies, waits for them, and re-layouts  6.23 us
    pallas_call x2, Pallas kernels, gather(): pl.pallas_call(kernel, in_specs=[pl.BlockSpec(memory_space=pltpu.SMEM), p...  5.28 us
    all_to_all x1, starting transfers between devices, local(): lax.all_to_all(message, 'grp', split_axis=0, concat_axis=0, tiled=True)  5.2 us
    reshape x3, local copies, waits for them, and re-layouts, exchange(): split = windows.reshape(-1, group, slots // group, channels)  3.27 us
    unnamed x20, other arithmetic  2.32 us
  transfers between devices with their start and end apart: 4, of which 3 were waited for; matrix products, arithmetic and copies ran while one was open for 20% of the time, Pallas kernels for 3%

profile of v1, /device:TPU:0, one launch (start us, length us, event | category | flops | bytes accessed | tf_op | source)
XLA Modules:
  0.0 86.4 jit_solution(12813662004722455369)
XLA Ops:
  0.0 0.7 broadcast_compare_fusion.1
  0.7 0.9 %convert_reduce_fusion = s32[16]{0:T(128)S(1)} fusion(s32[16]{0:T(128)} %param.12, pred[16]{0:T(512)(128)(4,1)S(1)} %broadcast_compare_fusion.1), kind=kLoop, calls=%fused_computation.121 | loop fusion | flops 1520 | bytes 144 | tf_op jit(solution)/shard_map/reduce_sum | solution.py:341
  1.6 0.7 broadcast_add_fusion.1
  2.3 0.8 fusion.45
  3.3 0.1 select_reduce_fusion
  3.5 0.7 pad_add_fusion
  4.1 5.2 %all-to-all-start = ((s32[8,1,70]{2,1,0:T(1,128)}), s32[8,1,70]{2,1,0:T(1,128)S(1)}, u32[]{:S(2)}, u32[]{:S(2)}) async-start(s32[8,1,70]{2,1,0:T(1,128)} %bitcast), calls=%async_computation | async-start | bytes 8192 | tf_op jit(solution)/shard_map/all_to_all | solution.py:354
  9.3 0.6 add_clamp_fusion
  9.9 1.0 %slice_bitcast_fusion = (bf16[3,64,64]{2,1,0:T(8,128)(2,1)S(1)}, bf16[3,64,64]{2,1,0:T(8,128)(2,1)S(1)}, bf16[3,64,64]{2,1,0:T(8,128)(2,1)S(1)}, bf16[3,64,64]{2...) fusion(bf16[3,3,3,64,64]{4,3,2,1,0:T(8,128)(2,1)} %param.10), kind=kLoop, calls=%fused_computation.92 | loop fusion | bytes 442368 | tf_op jit(solution)/shard_map/squeeze | solution.py:151
  11.0 1.0 %slice_bitcast_fusion.9 = (bf16[3,64,64]{2,1,0:T(8,128)(2,1)S(1)}, bf16[3,64,64]{2,1,0:T(8,128)(2,1)S(1)}, bf16[3,64,64]{2,1,0:T(8,128)(2,1)S(1)}, bf16[3,64,64]...) fusion(bf16[3,3,3,64,64]{4,3,2,1,0:T(8,128)(2,1)} %param.9), kind=kLoop, calls=%fused_computation.101 | loop fusion | bytes 442368 | tf_op jit(solution)/shard_map/squeeze | solution.py:151
  12.1 0.1 fusion.17
  12.2 0.1 fusion.23
  12.5 0.1 maximum_dynamic-update-slice_fusion.7
  12.6 0.1 fusion.18
  12.7 0.1 fusion.19
  12.9 0.1 maximum_dynamic-update-slice_fusion.2
  13.0 0.1 maximum_dynamic-update-slice_fusion.6
  13.1 0.1 fusion.11
  13.3 0.1 fusion.24
  14.0 0.1 fusion.13
  14.3 0.1 fusion.9
  14.7 0.7 copy-done.3
  15.3 0.2 broadcast_and_fusion
  15.5 0.4 and.510
  16.0 0.1 copy.98
  16.1 0.1 copy.99
  16.2 0.1 copy.100
  16.4 0.1 copy.101
  16.5 0.1 copy.102
  16.6 0.1 copy.103
  16.7 0.1 copy.104
  16.9 0.1 copy.105
  17.0 0.1 copy.106
  17.2 0.6 compare_bitcast_fusion.1
  18.1 0.2 broadcast_and_fusion.2
  18.3 0.4 and.482
  19.0 0.2 broadcast_and_fusion.1
  19.1 0.4 and.493
  20.0 2.2 %copy-done = bf16[4,64,64,128]{3,2,1,0:T(8,128)(2,1)S(1)} copy-done((bf16[4,64,64,128]{3,2,1,0:T(8,128)(2,1)S(1)}, bf16[4,64,64,128]{3,2,1,0:T(8,128)(2,1)}, u32[]{:S(2)}) %copy-start) | copy-done | bytes 4194328
  22.2 2.9 %shard_map.73 = (bf16[2,7,7,16,128]{4,3,2,1,0:T(8,128)(2,1)S(1)}, bf16[1,7,7,16,128]{4,3,2,1,0:T(8,128)(2,1)S(1)}) custom-call(s32[2,3,16]{2,1,0:T(4,128)S(1)} %pad_add_fusion.1.starts_ref, bf16[4,64,64,128]{3,2,1,0:T(8,128)(2,1)S(1)} %copy-done, bf16[2,2,112,256]{3,2,1,0:T(8,128)(2,1)S(1)} %add_convert_fusion.picks_ref), custom_call_target="tpu_custom_call" | custom-call | flops 100000000 | bytes 4000000 | tf_op jit(solution)/shard_map/pallas_call | solution.py:96
  25.1 0.8 copy.66
  25.9 4.2 %all-to-all-start.1 = ((bf16[49,8,2,128]{3,2,0,1:T(2,128)(2,1)}), bf16[49,8,2,128]{3,2,0,1:T(2,128)(2,1)S(1)}, u32[]{:S(2)}, u32[]{:S(2)}) async-start(bf16[49,8,2,128]{3,2,0,1:T(2,128)(2,1)} %copy.66), calls=%async_computation.1 | async-start | bytes 401408 | tf_op jit(solution)/shard_map/all_to_all | solution.py:317
  30.1 0.7 add_bitcast_fusion.2.starts_ref
  30.9 1.0 %copy.70 = bf16[98,8,2,128]{3,2,0,1:T(2,128)(2,1)} copy(bf16[98,8,2,128]{3,2,1,0:T(2,128)(2,1)S(1)} %bitcast.148) | data formatting | bytes 802816 | tf_op jit(solution)/shard_map/reshape | solution.py:316
  31.9 4.5 %all-to-all-done.1 = bf16[49,8,2,128]{3,2,0,1:T(2,128)(2,1)S(1)} async-done(((bf16[49,8,2,128]{3,2,0,1:T(2,128)(2,1)}), bf16[49,8,2,128]{3,2,0,1:T(2,128)(2,1)S(1)}, u32[]{:S(2)}, u32[]{:S(2)}) %all-to-all-start.1) | async-done | bytes 200736 | tf_op jit(solution)/shard_map/all_to_all | solution.py:317
  36.3 3.5 %all-to-all-start.3 = ((bf16[98,8,2,128]{3,2,0,1:T(2,128)(2,1)}), bf16[98,8,2,128]{3,2,0,1:T(2,128)(2,1)S(1)}, u32[]{:S(2)}, u32[]{:S(2)}) async-start(bf16[98,8,2,128]{3,2,0,1:T(2,128)(2,1)} %copy.70), calls=%async_computation.3 | async-start | bytes 802816 | tf_op jit(solution)/shard_map/all_to_all | solution.py:317
  39.9 0.7 stack.58
  40.8 2.2 %copy-done.1 = bf16[4,64,64,128]{3,2,1,0:T(8,128)(2,1)S(1)} copy-done((bf16[4,64,64,128]{3,2,1,0:T(8,128)(2,1)S(1)}, bf16[4,64,64,128]{3,2,1,0:T(8,128)(2,1)}, u32[]{:S(2)}) %copy-start.1) | copy-done | bytes 4194328
  43.0 2.4 %shard_map.74 = bf16[4,7,7,16,128]{4,3,2,1,0:T(8,128)(2,1)S(1)} custom-call(s32[1,3,16]{2,1,0:T(4,128)S(1)} %add_bitcast_fusion.2.starts_ref, bf16[4,64,64,128]{3,2,1,0:T(8,128)(2,1)S(1)} %copy-done.1, bf16[1,2,112,256]{3,2,1,0:T(8,128)(2,1)S(1)} %and_convert_fusion.picks_ref), custom_call_target="tpu_custom_call" | custom-call | flops 100000000 | bytes 4000000 | tf_op jit(solution)/shard_map/pallas_call | solution.py:96
  45.4 1.4 %copy.68 = bf16[196,8,2,128]{3,2,0,1:T(2,128)(2,1)} copy(bf16[196,8,2,128]{3,2,1,0:T(2,128)(2,1)S(1)} %bitcast.147) | data formatting | bytes 1605632 | tf_op jit(solution)/shard_map/reshape | solution.py:316
  46.8 1.3 %all-to-all-done.3 = bf16[98,8,2,128]{3,2,0,1:T(2,128)(2,1)S(1)} async-done(((bf16[98,8,2,128]{3,2,0,1:T(2,128)(2,1)}), bf16[98,8,2,128]{3,2,0,1:T(2,128)(2,1)S(1)}, u32[]{:S(2)}, u32[]{:S(2)}) %all-to-all-start.3) | async-done | bytes 401440 | tf_op jit(solution)/shard_map/all_to_all | solution.py:317
  48.1 3.7 %all-to-all-start.2 = ((bf16[196,8,2,128]{3,2,0,1:T(2,128)(2,1)}), bf16[196,8,2,128]{3,2,0,1:T(2,128)(2,1)S(1)}, u32[]{:S(2)}, u32[]{:S(2)}) async-start(bf16[196,8,2,128]{3,2,0,1:T(2,128)(2,1)} %copy.68), calls=%async_computation.2 | async-start | bytes 1605632 | tf_op jit(solution)/shard_map/all_to_all | solution.py:317
  51.9 0.7 pad_dynamic-update-slice_fusion
  52.6 1.3 %fusion.1.up_ref = bf16[3,512,256]{2,1,0:T(8,128)(2,1)} fusion(bf16[3,128,64]{2,1,0:T(8,128)(2,1)S(1)} %bitcast.160, bf16[3,128,64]{2,1,0:T(8,128)(2,1)S(1)} %bitcast.159, bf16[3,128,64]{2,1,0:T(8,128)(2,1)S(1)} %bitcast.158, bf16[3,128,64]{2,1,0:T(8,128)(2,1)S(1)} %bitcast.157, bf16[3,128,64]{2,1,0:T(8,128)(2,1)S(1)} %broadcast_in_dim.15, ...), kind=kLoop, calls=%fused_computation.2 | loop fusion | flops 10223616 | bytes 1540096 | tf_op jit(solution)/shard_map/concatenate | solution.py:134
  54.0 0.7 reshape.552.live_ref
  54.7 0.1 slice.191
  54.8 0.3 pad_maximum_fusion.33
  55.1 0.8 copy.67
  55.9 0.2 slice.192
  56.2 0.5 pad_maximum_fusion
  56.8 1.0 %copy.71 = bf16[98,8,2,128]{3,2,1,0:T(2,128)(2,1)} copy(bf16[98,8,2,128]{3,2,0,1:T(2,128)(2,1)S(1)} %pad_maximum_fusion) | data formatting | bytes 802816 | tf_op jit(solution)/shard_map/jit(_roll_static)/concatenate | solution.py:319
  57.8 6.6 %all-to-all-done.2 = bf16[196,8,2,128]{3,2,0,1:T(2,128)(2,1)S(1)} async-done(((bf16[196,8,2,128]{3,2,0,1:T(2,128)(2,1)}), bf16[196,8,2,128]{3,2,0,1:T(2,128)(2,1)S(1)}, u32[]{:S(2)}, u32[]{:S(2)}) %all-to-all-start.2) | async-done | bytes 802848 | tf_op jit(solution)/shard_map/all_to_all | solution.py:317
  64.4 1.5 %copy.69 = bf16[196,8,2,128]{3,2,1,0:T(2,128)(2,1)} copy(bf16[196,8,2,128]{3,2,0,1:T(2,128)(2,1)S(1)} %all-to-all-done.2) | data formatting | bytes 1605632 | tf_op jit(solution)/shard_map/all_to_all | solution.py:317
  65.8 20.5 %shard_map.75 = bf16[16,32768]{1,0:T(8,128)(2,1)} custom-call(bf16[1,7,7,16,128]{4,3,2,1,0:T(8,128)(2,1)} %bitcast.161, bf16[4,7,7,16,128]{4,3,2,1,0:T(8,128)(2,1)} %bitcast.150, bf16[2,7,7,16,128]{4,3,2,1,0:T(8,128)(2,1)} %bitcast.151, s32[16,27]{1,0:T(8,128)} %reshape.552.live_ref, bf16[3,512,256]{2,1,0:T(8,128)(2,1)} %fusion.1.up_ref, ...), custom_call_target="tpu_custom_call" | custom-call | flops 12000000000 | bytes 8000000 | tf_op jit(solution)/shard_map/pallas_call | solution.py:274
  (68 shorter events, 2.8 us)
Async XLA Ops:
  4.1 13.1 %all-to-all-start = ((s32[8,1,70]{2,1,0:T(1,128)}), s32[8,1,70]{2,1,0:T(1,128)S(1)}, u32[]{:S(2)}, u32[]{:S(2)}) async-start(s32[8,1,70]{2,1,0:T(1,128)} %bitcast), calls=%async_computation | async-start | bytes 8192 | tf_op jit(solution)/shard_map/all_to_all | solution.py:354
  13.3 1.4 %copy-start.2 = (bf16[3,3,3,128,64]{3,4,2,1,0:T(8,128)(2,1)S(1)}, bf16[3,3,3,128,64]{3,4,2,1,0:T(8,128)(2,1)}, u32[]{:S(2)}) copy-start(bf16[3,3,3,128,64]{3,4,2,1,0:T(8,128)(2,1)} %param.8) | copy-start | bytes 1327108
  14.2 1.2 %copy-start.3 = (bf16[3,1024,256]{2,1,0:T(8,128)(2,1)}, bf16[3,1024,256]{2,1,0:T(8,128)(2,1)S(1)}, u32[]{:S(2)}) copy-start(bf16[3,1024,256]{2,1,0:T(8,128)(2,1)S(1)} %get-tuple-element.52) | copy-start | bytes 4718596
  20.0 2.2 %copy-start = (bf16[4,64,64,128]{3,2,1,0:T(8,128)(2,1)S(1)}, bf16[4,64,64,128]{3,2,1,0:T(8,128)(2,1)}, u32[]{:S(2)}) copy-start(bf16[4,64,64,128]{3,2,1,0:T(8,128)(2,1)} %latents_ref.3) | copy-start | bytes 12582916
  25.9 10.4 %all-to-all-start.1 = ((bf16[49,8,2,128]{3,2,0,1:T(2,128)(2,1)}), bf16[49,8,2,128]{3,2,0,1:T(2,128)(2,1)S(1)}, u32[]{:S(2)}, u32[]{:S(2)}) async-start(bf16[49,8,2,128]{3,2,0,1:T(2,128)(2,1)} %copy.66), calls=%async_computation.1 | async-start | bytes 401408 | tf_op jit(solution)/shard_map/all_to_all | solution.py:317
  36.3 11.8 %all-to-all-start.3 = ((bf16[98,8,2,128]{3,2,0,1:T(2,128)(2,1)}), bf16[98,8,2,128]{3,2,0,1:T(2,128)(2,1)S(1)}, u32[]{:S(2)}, u32[]{:S(2)}) async-start(bf16[98,8,2,128]{3,2,0,1:T(2,128)(2,1)} %copy.70), calls=%async_computation.3 | async-start | bytes 802816 | tf_op jit(solution)/shard_map/all_to_all | solution.py:317
  39.9 5.5 %copy-start.4 = (bf16[3,1024,256]{2,1,0:T(8,128)(2,1)}, bf16[3,1024,256]{2,1,0:T(8,128)(2,1)S(1)}, u32[]{:S(2)}) copy-start(bf16[3,1024,256]{2,1,0:T(8,128)(2,1)S(1)} %pad_dynamic-update-slice_fusion.2) | copy-start | bytes 4718596
  40.8 2.2 %copy-start.1 = (bf16[4,64,64,128]{3,2,1,0:T(8,128)(2,1)S(1)}, bf16[4,64,64,128]{3,2,1,0:T(8,128)(2,1)}, u32[]{:S(2)}) copy-start(bf16[4,64,64,128]{3,2,1,0:T(8,128)(2,1)} %latents_ref.3) | copy-start | bytes 12582916
  48.1 16.2 %all-to-all-start.2 = ((bf16[196,8,2,128]{3,2,0,1:T(2,128)(2,1)}), bf16[196,8,2,128]{3,2,0,1:T(2,128)(2,1)S(1)}, u32[]{:S(2)}, u32[]{:S(2)}) async-start(bf16[196,8,2,128]{3,2,0,1:T(2,128)(2,1)} %copy.68), calls=%async_computation.2 | async-start | bytes 1605632 | tf_op jit(solution)/shard_map/all_to_all | solution.py:317

commit v2 on v0

v2 whole, which is shorter than its diff:
```python
import jax
import jax.numpy as jnp
from jax import lax
from jax.experimental import pallas as pl
from jax.experimental.pallas import tpu as pltpu
from jax.sharding import PartitionSpec as P


BE = 8
HB = 4
EDGE = HB + 3
WIN = 16
FAR = -1000
BIG = 65_536_000

EEDGE = BE + 4
HEDGE = BE + 2
EP = EEDGE // 2
HP = HEDGE // 2
OP = BE // 2

taps = (((1, 0),), ((2, 0), (0, 1)))

VMEM = pl.BlockSpec(memory_space=pltpu.VMEM)
SMEM = pl.BlockSpec(memory_space=pltpu.SMEM)
HBM = pl.BlockSpec(memory_space=pltpu.HBM)


def cost(flops, moved):
    return pl.CostEstimate(flops=flops, bytes_accessed=moved, transcendentals=0)


def window_of(brick, grid):
    across = grid // HB
    safe = jnp.maximum(brick, 0)
    along_y = lax.rem(lax.div(safe, across), across)
    low_y = along_y * HB - 1
    low_z = lax.rem(safe, across) * HB - 1
    start_y = jnp.clip(low_y, 0, grid - EDGE)
    start_z = jnp.clip(lax.div(low_z + 8, 8) * 8 - 8, 0, grid - WIN)
    return start_y, low_y - start_y, start_z, low_z - start_z, along_y == across - 1


def cut_windows(bricks, latents_ref, plane, count, win, sem, pick, out_ref, base):
    grid = latents_ref.shape[1]
    channels = latents_ref.shape[3]
    slots = len(bricks)
    group, _, capacity, _ = out_ref.shape
    places = [window_of(brick, grid) for brick in bricks]
    copies = []
    for slot, (start_y, _, start_z, _, _) in enumerate(places):
        copy = pltpu.make_async_copy(
            latents_ref.at[
                pl.ds(plane, count),
                pl.ds(start_y, EDGE),
                pl.ds(pl.multiple_of(start_z, 8), WIN),
                :,
            ],
            win.at[slot],
            sem.at[slot],
        )
        copy.start()
        copies.append(copy)

    def finish():
        shape = (EDGE * slots, slots * WIN)
        column = lax.broadcasted_iota(jnp.int32, (1, slots * WIN), 1)
        shift = jnp.full((1, slots * WIN), FAR, jnp.int32)
        late = shift
        for slot, (_, _, _, shift_z, top) in enumerate(places):
            here = column // WIN == slot
            value = jnp.where(bricks[slot] >= 0, shift_z, FAR)
            shift = jnp.where(here, value, shift)
            late = jnp.where(here, jnp.where(top, FAR, value), late)
        row = lax.broadcasted_iota(jnp.int32, shape, 0)
        column = lax.broadcasted_iota(jnp.int32, shape, 1)
        same = row % slots == column // WIN
        step = column % WIN - row // slots
        pick[0] = jnp.where(same & (step == shift), 1.0, 0.0).astype(jnp.bfloat16)
        pick[1] = jnp.where(same & (step == late), 1.0, 0.0).astype(jnp.bfloat16)
        for copy in copies:
            copy.wait()

        def line(y, carry):
            rows = [jnp.clip(y + place[1], 0, EDGE - 1) for place in places]
            planes = [
                jnp.concatenate([win[slot, x, rows[slot]] for slot in range(slots)], axis=0)
                for x in range(count)
            ]
            cut = jnp.dot(
                pick[(y >= EDGE - 2).astype(jnp.int32)],
                jnp.concatenate(planes, axis=1),
                preferred_element_type=jnp.float32,
            ).astype(jnp.bfloat16)
            for x in range(count):
                for z in range(EDGE):
                    out_ref[:, base + (x * EDGE + y) * EDGE + z] = cut[
                        z * slots : (z + 1) * slots, x * channels : (x + 1) * channels
                    ].reshape(group, capacity, channels)
            return carry

        lax.fori_loop(0, EDGE, line, 0)

    return finish


def gather_own(latents, brick_ids, brick_owner, neighbor_live, group, capacity):
    grid = latents.shape[1]
    channels = latents.shape[3]
    across = grid // HB
    listed = brick_ids.shape[0]
    slots = group * capacity
    cells = HB * EDGE * EDGE

    def kernel(ids_ref, owner_ref, near_ref, latents_ref, out_ref, ids_out, entry_of, used_by,
               flags, win, pick, sem):
        me = lax.axis_index("grp")
        for slot in range(slots):
            entry_of[slot] = -1
        for owner in range(group):
            used_by[owner] = 0
        for entry in range(listed):
            owner = jnp.clip(owner_ref[entry], 0, group - 1)
            rank = used_by[owner]

            @pl.when((ids_ref[entry] >= 0) & (rank < capacity))
            def _():
                entry_of[owner * capacity + rank] = entry
                used_by[owner] = rank + 1

        entries = [entry_of[slot] for slot in range(slots)]
        bricks = [
            jnp.where(entry >= 0, ids_ref[jnp.maximum(entry, 0)], -1) for entry in entries
        ]
        finish = cut_windows(bricks, latents_ref, 0, HB, win, sem, pick, out_ref, 0)

        lane = lax.broadcasted_iota(jnp.int32, (1, 128), 1)
        told = jnp.full((1, 128), -1, jnp.int32)
        for slot in range(slots):
            told = jnp.where(lane == slot, bricks[slot], told)
        for owner in range(group):
            ids_out[owner] = told

        offset = lax.broadcasted_iota(jnp.int32, (1, 27), 1)
        step_x = offset // 9 - 1
        step_y = offset // 3 % 3 - 1
        step_z = offset % 3 - 1
        inside_x = (me + step_x >= 0) & (me + step_x < group)
        flags[...] = jnp.zeros_like(flags)
        for slot in range(slots):
            safe = jnp.maximum(bricks[slot], 0)
            near_y = lax.rem(lax.div(safe, across), across) + step_y
            near_z = lax.rem(safe, across) + step_z
            inside = inside_x & (near_y >= 0) & (near_y < across)
            inside = inside & (near_z >= 0) & (near_z < across)
            near = near_ref[pl.ds(jnp.maximum(entries[slot], 0), 1), :]
            chosen = (near > 0) | (offset == 13)
            used = jnp.where(bricks[slot] >= 0, 1.0, 0.0)
            flags[slot : slot + 1, 0:27] = jnp.where(inside & chosen, used, 0.0)
        out_ref[:, cells] = flags[...].astype(jnp.bfloat16).reshape(group, capacity, channels)
        finish()

    return pl.pallas_call(
        kernel,
        in_specs=[SMEM, SMEM, VMEM, HBM],
        out_specs=[VMEM, VMEM],
        out_shape=[
            jax.ShapeDtypeStruct((group, cells + 1, capacity, channels), jnp.bfloat16),
            jax.ShapeDtypeStruct((group, 1, 128), jnp.int32),
        ],
        scratch_shapes=[
            pltpu.SMEM((slots,), jnp.int32),
            pltpu.SMEM((group,), jnp.int32),
            pltpu.VMEM((slots, 128), jnp.float32),
            pltpu.VMEM((slots, HB, EDGE, WIN, channels), jnp.bfloat16),
            pltpu.VMEM((2, EDGE * slots, slots * WIN), jnp.bfloat16),
            pltpu.SemaphoreType.DMA((slots,)),
        ],
        compiler_params=pltpu.CompilerParams(vmem_limit_bytes=BIG),
        cost_estimate=cost(1_000_000_000, 3_000_000),
    )(brick_ids, brick_owner, neighbor_live, latents)


def gather_rims(latents, heard, group, capacity):
    channels = latents.shape[3]
    slots = group * capacity
    plane_cells = EDGE * EDGE

    def kernel(heard_ref, latents_ref, out_ref, win_b, win_a, pick_b, pick_a, sem):
        me = lax.axis_index("grp")
        before = lax.rem(me + group - 1, group)
        after = lax.rem(me + 1, group)
        below = [jnp.where(me > 0, heard_ref[before, 0, slot], -1) for slot in range(slots)]
        above = [
            jnp.where(me < group - 1, heard_ref[after, 0, slot], -1) for slot in range(slots)
        ]
        finish_b = cut_windows(below, latents_ref, 0, 2, win_b, sem.at[0], pick_b, out_ref, 0)
        finish_a = cut_windows(
            above, latents_ref, HB - 1, 1, win_a, sem.at[1], pick_a, out_ref, 2 * plane_cells
        )
        finish_b()
        finish_a()

    return pl.pallas_call(
        kernel,
        in_specs=[SMEM, HBM],
        out_specs=VMEM,
        out_shape=jax.ShapeDtypeStruct(
            (group, 3 * plane_cells, capacity, channels), jnp.bfloat16
        ),
        scratch_shapes=[
            pltpu.VMEM((slots, 2, EDGE, WIN, channels), jnp.bfloat16),
            pltpu.VMEM((slots, 1, EDGE, WIN, channels), jnp.bfloat16),
            pltpu.VMEM((2, EDGE * slots, slots * WIN), jnp.bfloat16),
            pltpu.VMEM((2, EDGE * slots, slots * WIN), jnp.bfloat16),
            pltpu.SemaphoreType.DMA((2, slots)),
        ],
        compiler_params=pltpu.CompilerParams(vmem_limit_bytes=BIG),
        cost_estimate=cost(1_000_000_000, 3_000_000),
    )(heard, latents)


def pair_weights(up_weight, first_weight, second_weight, after):
    c1, c2 = up_weight.shape[3:]
    quad = 4 * c2
    lookup = {(parity, shift): tap for parity in (0, 1) for tap, shift in taps[parity]}

    def kernel(up_ref, first_ref, second_ref, after_ref, up_hbm, first_hbm, second_hbm,
               up_out, first_out, second_out, sem):
        moves = [
            pltpu.make_async_copy(source, target, sem.at[i])
            for i, (source, target) in enumerate(
                ((up_out, up_hbm), (first_out, first_hbm), (second_out, second_hbm))
            )
        ]
        for kx in range(3):
            for dy in (0, 1):
                for dz in (0, 1):
                    for py in (0, 1):
                        both = []
                        for pz in (0, 1):
                            ty = lookup.get((py, dy))
                            tz = lookup.get((pz, dz))
                            both.append(
                                jnp.zeros((c1, c2), jnp.bfloat16)
                                if ty is None or tz is None
                                else up_ref[kx, ty, tz]
                            )
                        at = (dy * 2 + dz) * c1
                        up_out[kx, at : at + c1, py * 2 * c2 : (py + 1) * 2 * c2] = (
                            jnp.concatenate(both, axis=1)
                        )
        moves[0].start()
        for raw, out, move in (
            (first_ref, first_out, moves[1]),
            (second_ref, second_out, moves[2]),
        ):
            def tile(kx, carry, raw=raw, out=out):
                for dy in (0, 1):
                    for dz in (0, 1):
                        for iy in (0, 1):
                            for iz in (0, 1):
                                for oy in (0, 1):
                                    both = []
                                    for oz in (0, 1):
                                        ky = 2 * dy + iy - oy
                                        kz = 2 * dz + iz - oz
                                        both.append(
                                            raw[kx, ky, kz]
                                            if 0 <= ky <= 2 and 0 <= kz <= 2
                                            else jnp.zeros((c2, c2), jnp.bfloat16)
                                        )
                                    at = (dy * 2 + dz) * quad + (iy * 2 + iz) * c2
                                    at = pl.multiple_of(kx * 4 * quad + at, c2)
                                    out[pl.ds(at, c2), oy * 2 * c2 : (oy + 1) * 2 * c2] = (
                                        jnp.concatenate(both, axis=1)
                                    )
                return carry

            lax.fori_loop(0, 3, tile, 0)
            move.start()
        for move in moves:
            move.wait()

    shapes = ((3, 4 * c1, quad), (12 * quad, quad), (12 * quad, quad))
    return pl.pallas_call(
        kernel,
        in_specs=[VMEM, VMEM, VMEM, HBM],
        out_specs=[HBM] * 3,
        out_shape=[jax.ShapeDtypeStruct(shape, jnp.bfloat16) for shape in shapes],
        scratch_shapes=[pltpu.VMEM(shape, jnp.bfloat16) for shape in shapes]
        + [pltpu.SemaphoreType.DMA((3,))],
        compiler_params=pltpu.CompilerParams(vmem_limit_bytes=BIG),
        cost_estimate=cost(1_000_000_000, 6_000_000),
    )(up_weight, first_weight, second_weight, after)


def pair_class(p):
    return 0 if p == 0 else 2 if p == EP - 1 else 1


def cell_class(h):
    return 0 if h == 0 else 2 if h == HEDGE - 1 else 1


class Decoder:
    def __init__(self, slots, c1, quad):
        self.slots, self.c1, self.quad = slots, c1, quad

    def scratch(self):
        slots, quad = self.slots, self.quad
        return [
            pltpu.VMEM((EDGE, EDGE, EDGE, slots, self.c1), jnp.bfloat16),
            pltpu.VMEM((EEDGE, EP, EP, slots, quad), jnp.bfloat16),
            pltpu.VMEM((HEDGE, HP, HP, slots, quad), jnp.bfloat16),
            pltpu.VMEM((3, EP, EP, slots, quad // 2), jnp.bfloat16),
            pltpu.VMEM((3, HP, HP, slots, quad), jnp.bfloat16),
            pltpu.VMEM((slots, self.c1), jnp.float32),
            pltpu.VMEM((3, 4 * self.c1, quad), jnp.bfloat16),
            pltpu.VMEM((12 * quad, quad), jnp.bfloat16),
            pltpu.VMEM((12 * quad, quad), jnp.bfloat16),
            pltpu.SemaphoreType.DMA((3,)),
        ]

    @staticmethod
    def fetch(sources, targets, sem):
        moves = [
            pltpu.make_async_copy(source, target, sem.at[i])
            for i, (source, target) in enumerate(zip(sources, targets))
        ]
        for move in moves:
            move.start()
        return moves

    def masks(self, flags, emask, hmask, classes):
        half, c2 = self.quad // 2, self.quad // 4
        wide = {
            cx * 9 + n: jnp.broadcast_to(flags[:, cx * 9 + n : cx * 9 + n + 1], (self.slots, half))
            for cx in classes
            for n in range(9)
        }
        left = lax.broadcasted_iota(jnp.int32, (self.slots, half), 1) < c2
        for cx in classes:
            for py in range(EP):
                for pz in range(EP):
                    n = cx * 9 + pair_class(py) * 3 + pair_class(pz)
                    emask[cx, py, pz] = wide[n].astype(jnp.bfloat16)
            mixed = {}
            for py in range(HP):
                for pz in range(HP):
                    for ty in (0, 1):
                        n = cx * 9 + cell_class(2 * py + ty) * 3
                        key = (n + cell_class(2 * pz), n + cell_class(2 * pz + 1))
                        if key not in mixed:
                            mixed[key] = jnp.where(left, wide[key[0]], wide[key[1]]).astype(
                                jnp.bfloat16
                            )
                        hmask[cx, py, pz, :, ty * half : (ty + 1) * half] = mixed[key]

    def patch(self, reg, x):
        return jnp.concatenate(
            [
                reg[x, dy : dy + EP, dz : dz + EP].reshape(-1, self.c1)
                for dy in (0, 1)
                for dz in (0, 1)
            ],
            axis=1,
        )

    def raise_cells(self, reg, up_ref, emask, ext, px, parities):
        cx = jnp.where(px == 0, 0, jnp.where(px == EP - 1, 2, 1))
        mask = emask[cx].reshape(-1, self.quad // 2)
        mask = jnp.concatenate([mask, mask], axis=1)
        shape = (EP, EP, self.slots, self.quad)
        near = self.patch(reg, px)
        if 0 in parities:
            even = jnp.dot(near, up_ref[1], preferred_element_type=jnp.float32)
            ext[2 * px] = (even.astype(jnp.bfloat16) * mask).reshape(shape)
        if 1 in parities:
            odd = jnp.dot(near, up_ref[2], preferred_element_type=jnp.float32)
            odd += jnp.dot(self.patch(reg, px + 1), up_ref[0], preferred_element_type=jnp.float32)
            ext[2 * px + 1] = (odd.astype(jnp.bfloat16) * mask).reshape(shape)

    def conv(self, source, x, pairs, weight_ref):
        pieces = [
            source[x + kx, dy : dy + pairs, dz : dz + pairs].reshape(-1, self.quad)
            for kx in range(3)
            for dy in (0, 1)
            for dz in (0, 1)
        ]
        return jnp.dot(
            jnp.concatenate(pieces, axis=1), weight_ref[...], preferred_element_type=jnp.float32
        )

    def hide(self, ext, first_ref, hmask, hid, x):
        value = self.conv(ext, x, HP, first_ref)
        cx = jnp.where(x == 0, 0, jnp.where(x == HEDGE - 1, 2, 1))
        value = (value * (1.0 / (1.0 + jnp.exp(-value)))).astype(jnp.bfloat16)
        value = value * hmask[cx].reshape(-1, self.quad)
        hid[x] = value.reshape(HP, HP, self.slots, self.quad)

    def refine(self, ext, hid, second_ref, rows, x, at):
        half = self.quad // 2
        value = self.conv(hid, x, OP, second_ref)
        centre = ext[x + 2, 1 : 1 + OP, 1 : 1 + OP].reshape(-1, self.quad)
        value = (value + centre.astype(jnp.float32)).astype(jnp.bfloat16)
        value = value.reshape(OP, OP, self.slots, self.quad)
        for py in range(OP):
            for ty in (0, 1):
                line = jnp.concatenate(
                    [value[py, pz, :, ty * half : (ty + 1) * half] for pz in range(OP)], axis=1
                )
                start = pl.multiple_of(at * BE * OP * half + (2 * py + ty) * OP * half, 128)
                rows[:, pl.ds(start, OP * half)] = line


INNER_H, INNER_O = (2, 7), (2, 5)
KEPT_E = (2, 3, 7, 8)
KEPT_H = (2, 3, 5, 6)


def decode_inner(own, up_pairs, first_pairs, second_pairs):
    group, _, capacity, c1 = own.shape
    quad = up_pairs.shape[2]
    slots = group * capacity
    plane = BE * BE * quad // 4
    steps = Decoder(slots, c1, quad)
    width = (INNER_O[1] - INNER_O[0]) * plane

    def kernel(own_ref, up_in, first_in, second_in, out_ref, ext_out, hid_out,
               reg, ext, hid, emask, hmask, flags, up_ref, first_ref, second_ref, wsem, rows, sem):
        weights = steps.fetch(
            (up_in, first_in, second_in), (up_ref, first_ref, second_ref), wsem
        )
        flags[...] = own_ref[:, HB * EDGE * EDGE].reshape(slots, c1).astype(jnp.float32)

        def load(y, carry):
            for x in range(HB):
                for z in range(EDGE):
                    reg[1 + x, y, z] = own_ref[:, (x * EDGE + y) * EDGE + z].reshape(slots, c1)
            return carry

        lax.fori_loop(0, EDGE, load, 0)
        steps.masks(flags, emask, hmask, (1,))
        weights[0].wait()

        def both(px, carry):
            steps.raise_cells(reg, up_ref, emask, ext, px, (0, 1))
            return carry

        lax.fori_loop(1, HB, both, 0)
        steps.raise_cells(reg, up_ref, emask, ext, HB, (0,))
        copies = [
            pltpu.make_async_copy(ext.at[e], ext_out.at[i], sem.at[i])
            for i, e in enumerate(KEPT_E)
        ]
        for copy in copies:
            copy.start()

        weights[1].wait()

        def hide(x, carry):
            steps.hide(ext, first_ref, hmask, hid, x)
            return carry

        lax.fori_loop(INNER_H[0], INNER_H[1], hide, 0)
        more = [
            pltpu.make_async_copy(hid.at[h], hid_out.at[i], sem.at[4 + i])
            for i, h in enumerate(KEPT_H)
        ]
        for copy in more:
            copy.start()

        weights[2].wait()

        def refine(x, carry):
            steps.refine(ext, hid, second_ref, rows, x, x - INNER_O[0])
            return carry

        lax.fori_loop(INNER_O[0], INNER_O[1], refine, 0)
        last = pltpu.make_async_copy(
            rows, out_ref.at[:, pl.ds(INNER_O[0] * plane, width)], sem.at[8]
        )
        last.start()
        for copy in copies + more + [last]:
            copy.wait()

    return pl.pallas_call(
        kernel,
        in_specs=[VMEM] + [HBM] * 3,
        out_specs=[HBM] * 3,
        out_shape=[
            jax.ShapeDtypeStruct((slots, BE * plane), jnp.bfloat16),
            jax.ShapeDtypeStruct((len(KEPT_E), EP, EP, slots, quad), jnp.bfloat16),
            jax.ShapeDtypeStruct((len(KEPT_H), HP, HP, slots, quad), jnp.bfloat16),
        ],
        scratch_shapes=steps.scratch()
        + [pltpu.VMEM((slots, width), jnp.bfloat16), pltpu.SemaphoreType.DMA((9,))],
        compiler_params=pltpu.CompilerParams(vmem_limit_bytes=64_000_000),
        cost_estimate=cost(8_000_000_000, 6_000_000),
    )(own, up_pairs, first_pairs, second_pairs)


def decode_outer(own, rims, out, ext_kept, hid_kept, up_pairs, first_pairs, second_pairs):
    group, _, capacity, c1 = own.shape
    quad = up_pairs.shape[2]
    slots = group * capacity
    plane = BE * BE * quad // 4
    steps = Decoder(slots, c1, quad)
    plane_cells = EDGE * EDGE
    low_o = INNER_O[0]
    high_o = BE - INNER_O[1]

    def kernel(own_ref, rims_ref, up_in, first_in, second_in, ext_in, hid_in, out_in, out_ref,
               reg, ext, hid, emask, hmask, flags, up_ref, first_ref, second_ref, wsem, rows, sem):
        weights = steps.fetch(
            (up_in, first_in, second_in), (up_ref, first_ref, second_ref), wsem
        )
        copies = [
            pltpu.make_async_copy(ext_in.at[i], ext.at[e], sem.at[i])
            for i, e in enumerate(KEPT_E)
        ] + [
            pltpu.make_async_copy(hid_in.at[i], hid.at[h], sem.at[4 + i])
            for i, h in enumerate(KEPT_H)
        ]
        for copy in copies:
            copy.start()
        flags[...] = own_ref[:, HB * plane_cells].reshape(slots, c1).astype(jnp.float32)

        def turned(row, shift):
            value = rims_ref[:, row].reshape(slots, c1)
            cut = (shift % group) * capacity
            return jnp.concatenate([value[cut:], value[:cut]], axis=0)

        def load(y, carry):
            for z in range(EDGE):
                at = y * EDGE + z
                reg[0, y, z] = turned(2 * plane_cells + at, -1)
                reg[1, y, z] = own_ref[:, at].reshape(slots, c1)
                reg[HB, y, z] = own_ref[:, (HB - 1) * plane_cells + at].reshape(slots, c1)
                reg[HB + 1, y, z] = turned(at, 1)
                reg[HB + 2, y, z] = turned(plane_cells + at, 1)
            return carry

        lax.fori_loop(0, EDGE, load, 0)
        steps.masks(flags, emask, hmask, (0, 1, 2))
        weights[0].wait()

        def both(i, carry):
            steps.raise_cells(reg, up_ref, emask, ext, i * (EP - 1), (0, 1))
            return carry

        lax.fori_loop(0, 2, both, 0)
        steps.raise_cells(reg, up_ref, emask, ext, HB, (1,))
        for copy in copies:
            copy.wait()

        weights[1].wait()

        def hide(i, carry):
            x = jnp.where(i < INNER_H[0], i, i + INNER_H[1] - INNER_H[0])
            steps.hide(ext, first_ref, hmask, hid, x)
            return carry

        lax.fori_loop(0, HEDGE - INNER_H[1] + INNER_H[0], hide, 0)

        weights[2].wait()

        def refine(i, carry):
            x = jnp.where(i < low_o, i, i + INNER_O[1] - low_o)
            steps.refine(ext, hid, second_ref, rows, x, i)
            return carry

        lax.fori_loop(0, low_o + high_o, refine, 0)
        ends = [
            pltpu.make_async_copy(
                rows.at[:, pl.ds(0, low_o * plane)], out_ref.at[:, pl.ds(0, low_o * plane)],
                sem.at[8],
            ),
            pltpu.make_async_copy(
                rows.at[:, pl.ds(low_o * plane, high_o * plane)],
                out_ref.at[:, pl.ds(INNER_O[1] * plane, high_o * plane)],
                sem.at[9],
            ),
        ]
        for copy in ends:
            copy.start()
        for copy in ends:
            copy.wait()

    return pl.pallas_call(
        kernel,
        in_specs=[VMEM] * 2 + [HBM] * 6,
        out_specs=HBM,
        out_shape=jax.ShapeDtypeStruct((slots, BE * plane), jnp.bfloat16),
        scratch_shapes=steps.scratch()
        + [
            pltpu.VMEM((slots, (low_o + high_o) * plane), jnp.bfloat16),
            pltpu.SemaphoreType.DMA((10,)),
        ],
        input_output_aliases={7: 0},
        compiler_params=pltpu.CompilerParams(vmem_limit_bytes=64_000_000),
        cost_estimate=cost(8_000_000_000, 6_000_000),
    )(own, rims, up_pairs, first_pairs, second_pairs, ext_kept, hid_kept, out)


def to_owners(array):
    return lax.all_to_all(array, "grp", split_axis=0, concat_axis=0, tiled=True)


def local(latents, up_weight, first_weight, second_weight, brick_ids, brick_owner, neighbor_live):
    group = lax.axis_size("grp")
    capacity = max(2, brick_ids.shape[0] // group)
    assert latents.shape[0] == HB
    own, told = gather_own(
        latents, brick_ids, brick_owner, neighbor_live, group, capacity
    )
    own = to_owners(own)
    heard = to_owners(told)
    rims = gather_rims(latents, heard, group, capacity)
    rims = to_owners(rims)
    pairs = pair_weights(up_weight, first_weight, second_weight, heard)
    out, ext_kept, hid_kept = decode_inner(own, *pairs)
    return decode_outer(own, rims, out, ext_kept, hid_kept, *pairs)


def solution(mesh):
    in_specs = (
        P(("shape", "grp"), None, None, None),
        P(),
        P(),
        P(),
        P(("shape", "grp")),
        P(("shape", "grp")),
        P(("shape", "grp"), None),
    )
    out_specs = P(("shape", "grp"), None)
    return jax.shard_map(local, mesh=mesh, in_specs=in_specs, out_specs=out_specs, check_vma=False)
```

time: 394 us -> 60.3 us (0.15)
  matrix products: 181 us -> 0 us
  local copies, waits for them, and re-layouts: 104 us -> 2.06 us
  blocking collectives: 58.1 us -> 9.9 us
  other arithmetic: 43.7 us -> 0 us
  Pallas kernels: 0 us -> 40.4 us
    conv_general_dilated x2 -> x0, matrix products: 173 us -> none  [conv_valid(): lax.conv_general_dilated(inputs, kernel, (1, 1, 1), 'VALID', dimension_nu...]
    gather x49 -> x0, local copies, waits for them, and re-layouts: 67.9 us -> none
    all_to_all x1, blocking collectives: 58.1 us -> 9.9 us  [to_owners(): return lax.all_to_all(array, 'grp', split_axis=0, concat_axis=0, tiled=True)]
    pallas_call x0 -> x5, Pallas kernels: none -> 40.4 us  [the longest x1 12.6 us: decode_outer(): pl.pallas_call(kernel, in_specs=[VMEM] * 2 + [HBM] * 6, out_specs=HBM, ou...]
    another operation x6 -> x0, other arithmetic: 22.6 us -> none  [the longest x3 20.5 us: upsample(): alternated = jnp.stack(parity_grids, axis=2)]
    concatenate x2 -> x0, other arithmetic: 12.4 us -> none  [the longest x1 12.4 us: extended_2(): block = jnp.concatenate([low, block, high], axis=dim)]
    another operation x1 -> x0, local copies, waits for them, and re-layouts: 12.1 us -> none  [upsample(): alternated = jnp.stack(parity_grids, axis=2)]
    slice x4 -> x0, local copies, waits for them, and re-layouts: 11.5 us -> none  [the longest x1 5.18 us: extended_2(): lax.slice_in_dim(block, block.shape[dim] - width, None, axis=dim)]
  transfers between devices with their start and end apart: 2 -> 2, of which waited for: 0 -> 1; matrix products, arithmetic and copies ran while one was open for 2% -> 2% of each run, Pallas kernels for 0% -> 38%
where the time goes in v2:
time: 60.3 us; the launch traced here: 59.7 us
  Pallas kernels  40.4 us (67%)
  blocking collectives  9.9 us (16%)
  starting transfers between devices  7.09 us (12%)
  local copies, waits for them, and re-layouts  2.06 us (3%)
    pallas_call x1, Pallas kernels, decode_outer(): pl.pallas_call(kernel, in_specs=[VMEM] * 2 + [HBM] * 6, out_specs=HBM, ou...  12.6 us
    pallas_call x1, Pallas kernels, decode_inner(): pl.pallas_call(kernel, in_specs=[VMEM] + [HBM] * 3, out_specs=[HBM] * 3,...  11.2 us
    all_to_all x1, blocking collectives, to_owners(): return lax.all_to_all(array, 'grp', split_axis=0, concat_axis=0, tiled=True)  9.9 us
    pallas_call x1, Pallas kernels, gather_rims(): pl.pallas_call(kernel, in_specs=[SMEM, HBM], out_specs=VMEM, out_shape=ja...  7.54 us
    all_to_all x2, starting transfers between devices, to_owners(): return lax.all_to_all(array, 'grp', split_axis=0, concat_axis=0, tiled=True)  7.09 us
    pallas_call x1, Pallas kernels, gather_own(): pl.pallas_call(kernel, in_specs=[SMEM, SMEM, VMEM, HBM], out_specs=[VMEM,...  5.29 us
    pallas_call x1, Pallas kernels, pair_weights(): pl.pallas_call(kernel, in_specs=[VMEM, VMEM, VMEM, HBM], out_specs=[HBM]...  3.74 us
    unnamed x7, local copies, waits for them, and re-layouts  2.06 us
  transfers between devices with their start and end apart: 2, of which 1 were waited for; matrix products, arithmetic and copies ran while one was open for 2% of the time, Pallas kernels for 38%

profile of v2, /device:TPU:0, one launch (start us, length us, event | category | flops | bytes accessed | tf_op | source)
XLA Modules:
  0.0 59.7 jit_solution(3975867251898048382)
XLA Ops:
  0.0 5.3 %shard_map.73 = (bf16[8,197,2,128]{3,2,1,0:T(2,128)(2,1)}, s32[8,1,128]{2,1,0:T(1,128)}) custom-call(s32[16]{0:T(128)} %ids_ref.1, s32[16]{0:T(128)} %owner_ref.1, s32[16,27]{1,0:T(8,128)} %near_ref.1, bf16[4,64,64,128]{3,2,1,0:T(8,128)(2,1)} %latents_ref.3), custom_call_target="tpu_custom_call" | custom-call | flops 1000000000 | bytes 3000000 | tf_op jit(solution)/shard_map/pallas_call | solution.py:163
  5.3 0.0 copy-start.2
  5.3 9.9 %all_to_all.15.heard_ref.after_ref = s32[8,1,128]{2,1,0:T(1,128)} all-to-all(s32[8,1,128]{2,1,0:T(1,128)} %get-tuple-element.14), channel_id=1, replica_groups=mesh['shape'=4,'grp'=8] {'grp'}, dimensions={0} | all-to-all | bytes 8192 | tf_op jit(solution)/shard_map/all_to_all | solution.py:608
  15.2 3.5 %all-to-all-start = ((bf16[8,197,2,128]{3,2,1,0:T(2,128)(2,1)}), bf16[8,197,2,128]{3,2,1,0:T(2,128)(2,1)S(1)}, u32[]{:S(2)}, u32[]{:S(2)}) async-start(bf16[8,197,2,128]{3,2,1,0:T(2,128)(2,1)} %get-tuple-element.13), calls=%async_computation | async-start | bytes 1613824 | tf_op jit(solution)/shard_map/all_to_all | solution.py:608
  18.8 0.0 copy-done.2
  18.8 1.2 %copy.9.up_ref = bf16[3,3,3,128,64]{4,3,2,1,0:T(8,128)(2,1)} copy(bf16[3,3,3,128,64]{3,4,2,1,0:T(8,128)(2,1)S(1)} %copy-done.2) | data formatting | bytes 884736 | tf_op args[1]
  20.0 7.5 %shard_map.74 = bf16[8,147,2,128]{3,2,1,0:T(2,128)(2,1)} custom-call(s32[8,1,128]{2,1,0:T(1,128)} %all_to_all.15.heard_ref.after_ref, bf16[4,64,64,128]{3,2,1,0:T(8,128)(2,1)} %latents_ref.3), custom_call_target="tpu_custom_call" | custom-call | flops 1000000000 | bytes 3000000 | tf_op jit(solution)/shard_map/pallas_call | solution.py:204
  27.5 3.7 %shard_map.75 = (bf16[3,512,256]{2,1,0:T(8,128)(2,1)}, bf16[3072,256]{1,0:T(8,128)(2,1)}, bf16[3072,256]{1,0:T(8,128)(2,1)}) custom-call(bf16[3,3,3,128,64]{4,3,2,1,0:T(8,128)(2,1)} %copy.9.up_ref, bf16[3,3,3,64,64]{4,3,2,1,0:T(8,128)(2,1)} %first_ref.1, bf16[3,3,3,64,64]{4,3,2,1,0:T(8,128)(2,1)} %second_ref.1, s32[8,1,128]{2,1,0:T(1,128)} %all_to_all.15.heard_ref.after_ref), custom_call_target="tpu_custom_call" | custom-call | flops 1000000000 | bytes 6000000 | tf_op jit(solution)/shard_map/pallas_call | solution.py:286
  31.3 0.2 all-to-all-done.own_ref
  31.5 0.0 copy-start
  31.5 3.5 %all-to-all-start.2 = ((bf16[8,147,2,128]{3,2,1,0:T(2,128)(2,1)}), bf16[8,147,2,128]{3,2,1,0:T(2,128)(2,1)S(1)}, u32[]{:S(2)}, u32[]{:S(2)}) async-start(bf16[8,147,2,128]{3,2,1,0:T(2,128)(2,1)} %shard_map.74), calls=%async_computation.2 | async-start | bytes 1204224 | tf_op jit(solution)/shard_map/all_to_all | solution.py:608
  35.0 0.0 copy-done
  35.0 11.2 %shard_map.76 = (bf16[16,32768]{1,0:T(8,128)(2,1)}, bf16[4,6,6,16,256]{4,3,2,1,0:T(8,128)(2,1)}, bf16[4,5,5,16,256]{4,3,2,1,0:T(8,128)(2,1)}) custom-call(bf16[8,197,2,128]{3,2,1,0:T(2,128)(2,1)} %copy-done, bf16[3,512,256]{2,1,0:T(8,128)(2,1)} %get-tuple-element.15.up_in, bf16[3072,256]{1,0:T(8,128)(2,1)} %get-tuple-element.16.first_in, ...), custom_call_target="tpu_custom_call" | custom-call | flops 8000000000 | bytes 6000000 | tf_op jit(solution)/shard_map/pallas_call | solution.py:488
  46.3 0.0 all-to-all-done.2.rims_ref
  46.3 0.0 copy-start.1
  46.3 0.8 %copy-done.1 = bf16[8,147,2,128]{3,2,1,0:T(2,128)(2,1)} copy-done((bf16[8,147,2,128]{3,2,1,0:T(2,128)(2,1)}, bf16[8,147,2,128]{3,2,1,0:T(2,128)(2,1)S(1)}, u32[]{:S(2)}) %copy-start.1) | copy-done | bytes 602136
  47.1 12.6 %shard_map.77 = bf16[16,32768]{1,0:T(8,128)(2,1)} custom-call(bf16[8,197,2,128]{3,2,1,0:T(2,128)(2,1)} %copy-done, bf16[8,147,2,128]{3,2,1,0:T(2,128)(2,1)} %copy-done.1, bf16[3,512,256]{2,1,0:T(8,128)(2,1)} %get-tuple-element.15.up_in, bf16[3072,256]{1,0:T(8,128)(2,1)} %get-tuple-element.16.first_in, ...), custom_call_target="tpu_custom_call", output_to_operand_aliasing={{}: (7, {})} | custom-call | flops 8000000000 | bytes 6000000 | tf_op jit(solution)/shard_map/pallas_call | solution.py:591
Async XLA Ops:
  5.3 13.5 %copy-start.2 = (bf16[3,3,3,128,64]{3,4,2,1,0:T(8,128)(2,1)S(1)}, bf16[3,3,3,128,64]{3,4,2,1,0:T(8,128)(2,1)}, u32[]{:S(2)}) copy-start(bf16[3,3,3,128,64]{3,4,2,1,0:T(8,128)(2,1)} %param.8) | copy-start | bytes 1327108
  15.2 16.3 %all-to-all-start = ((bf16[8,197,2,128]{3,2,1,0:T(2,128)(2,1)}), bf16[8,197,2,128]{3,2,1,0:T(2,128)(2,1)S(1)}, u32[]{:S(2)}, u32[]{:S(2)}) async-start(bf16[8,197,2,128]{3,2,1,0:T(2,128)(2,1)} %get-tuple-element.13), calls=%async_computation | async-start | bytes 1613824 | tf_op jit(solution)/shard_map/all_to_all | solution.py:608
  31.5 3.6 %copy-start = (bf16[8,197,2,128]{3,2,1,0:T(2,128)(2,1)}, bf16[8,197,2,128]{3,2,1,0:T(2,128)(2,1)S(1)}, u32[]{:S(2)}) copy-start(bf16[8,197,2,128]{3,2,1,0:T(2,128)(2,1)S(1)} %all-to-all-done.own_ref) | copy-start | bytes 2420740
  31.5 14.8 %all-to-all-start.2 = ((bf16[8,147,2,128]{3,2,1,0:T(2,128)(2,1)}), bf16[8,147,2,128]{3,2,1,0:T(2,128)(2,1)S(1)}, u32[]{:S(2)}, u32[]{:S(2)}) async-start(bf16[8,147,2,128]{3,2,1,0:T(2,128)(2,1)} %shard_map.74), calls=%async_computation.2 | async-start | bytes 1204224 | tf_op jit(solution)/shard_map/all_to_all | solution.py:608
  46.3 0.8 %copy-start.1 = (bf16[8,147,2,128]{3,2,1,0:T(2,128)(2,1)}, bf16[8,147,2,128]{3,2,1,0:T(2,128)(2,1)S(1)}, u32[]{:S(2)}) copy-start(bf16[8,147,2,128]{3,2,1,0:T(2,128)(2,1)S(1)} %all-to-all-done.2.rims_ref) | copy-start | bytes 1806340

commit v3 on v2

--- a/solution.py
+++ b/solution.py
@@ -12,6 +12,7 @@
 WIN = 16
 FAR = -1000
 BIG = 65_536_000
+WEIGHT_ROWS = 36_864
 
 EEDGE = BE + 4
 HEDGE = BE + 2
@@ -30,25 +31,52 @@
     return pl.CostEstimate(flops=flops, bytes_accessed=moved, transcendentals=0)
 
 
+def parts(value, size):
+    if size & (size - 1):
+        return lax.div(value, size), lax.rem(value, size)
+    return value >> (size.bit_length() - 1), value & (size - 1)
+
+
+def brick_place(brick, across):
+    rest, along_z = parts(jnp.maximum(brick, 0), across)
+    return parts(rest, across)[1], along_z
+
+
 def window_of(brick, grid):
     across = grid // HB
-    safe = jnp.maximum(brick, 0)
-    along_y = lax.rem(lax.div(safe, across), across)
+    along_y, along_z = brick_place(brick, across)
     low_y = along_y * HB - 1
-    low_z = lax.rem(safe, across) * HB - 1
+    low_z = along_z * HB - 1
     start_y = jnp.clip(low_y, 0, grid - EDGE)
-    start_z = jnp.clip(lax.div(low_z + 8, 8) * 8 - 8, 0, grid - WIN)
+    start_z = jnp.clip(((low_z + 8) & -8) - 8, 0, grid - WIN)
     return start_y, low_y - start_y, start_z, low_z - start_z, along_y == across - 1
 
 
-def cut_windows(bricks, latents_ref, plane, count, win, sem, pick, out_ref, base):
+def spread(values, group_of, blank):
+    row = jnp.full(group_of.shape, blank, jnp.int32)
+    for entry, value in enumerate(values):
+        row = jnp.where(group_of == entry, value, row)
+    return row
+
+
+def slot_targets(bricks, owners, capacity, group_of):
+    owners = [jnp.where(brick >= 0, owner, -1) for brick, owner in zip(bricks, owners)]
+    owner_row = spread(owners, group_of, -1)
+    rank = jnp.zeros_like(owner_row)
+    for entry, owner in enumerate(owners):
+        rank += jnp.where((group_of > entry) & (owner_row == owner), 1, 0)
+    return jnp.where(owner_row >= 0, owner_row * capacity + rank, -1)
+
+
+def cut_windows(bricks, owners, latents_ref, plane, count, win, sem, pick, out_ref, base):
     grid = latents_ref.shape[1]
     channels = latents_ref.shape[3]
-    slots = len(bricks)
+    listed = len(bricks)
     group, _, capacity, _ = out_ref.shape
+    slots = group * capacity
     places = [window_of(brick, grid) for brick in bricks]
     copies = []
-    for slot, (start_y, _, start_z, _, _) in enumerate(places):
+    for entry, (start_y, _, start_z, _, _) in enumerate(places):
         copy = pltpu.make_async_copy(
             latents_ref.at[
                 pl.ds(plane, count),
@@ -56,35 +84,30 @@
                 pl.ds(pl.multiple_of(start_z, 8), WIN),
                 :,
             ],
-            win.at[slot],
-            sem.at[slot],
+            win.at[entry],
+            sem.at[entry],
         )
         copy.start()
         copies.append(copy)
+    column = lax.broadcasted_iota(jnp.int32, (1, listed * WIN), 1)
+    group_of, cell = parts(column, WIN)
+    target = slot_targets(bricks, owners, capacity, group_of)
 
     def finish():
-        shape = (EDGE * slots, slots * WIN)
-        column = lax.broadcasted_iota(jnp.int32, (1, slots * WIN), 1)
-        shift = jnp.full((1, slots * WIN), FAR, jnp.int32)
-        late = shift
-        for slot, (_, _, _, shift_z, top) in enumerate(places):
-            here = column // WIN == slot
-            value = jnp.where(bricks[slot] >= 0, shift_z, FAR)
-            shift = jnp.where(here, value, shift)
-            late = jnp.where(here, jnp.where(top, FAR, value), late)
-        row = lax.broadcasted_iota(jnp.int32, shape, 0)
-        column = lax.broadcasted_iota(jnp.int32, shape, 1)
-        same = row % slots == column // WIN
-        step = column % WIN - row // slots
-        pick[0] = jnp.where(same & (step == shift), 1.0, 0.0).astype(jnp.bfloat16)
-        pick[1] = jnp.where(same & (step == late), 1.0, 0.0).astype(jnp.bfloat16)
+        shape = (EDGE * slots, listed * WIN)
+        shift = spread([place[3] for place in places], group_of, FAR)
+        late = spread([jnp.where(place[4], FAR, place[3]) for place in places], group_of, FAR)
+        step, at = parts(lax.broadcasted_iota(jnp.int32, shape, 0), slots)
+        same = at == target
+        pick[0] = jnp.where(same & (step == cell - shift), 1.0, 0.0).astype(jnp.bfloat16)
+        pick[1] = jnp.where(same & (step == cell - late), 1.0, 0.0).astype(jnp.bfloat16)
         for copy in copies:
             copy.wait()
 
         def line(y, carry):
             rows = [jnp.clip(y + place[1], 0, EDGE - 1) for place in places]
             planes = [
-                jnp.concatenate([win[slot, x, rows[slot]] for slot in range(slots)], axis=0)
+                jnp.concatenate([win[entry, x, rows[entry]] for entry in range(listed)], axis=0)
                 for x in range(count)
             ]
             cut = jnp.dot(
@@ -99,9 +122,9 @@
                     ].reshape(group, capacity, channels)
             return carry
 
-        lax.fori_loop(0, EDGE, line, 0)
-
-    return finish
+        lax.fori_loop(0, EDGE, line, 0, unroll=True)
+
+    return target, cell, finish
 
 
 def gather_own(latents, brick_ids, brick_owner, neighbor_live, group, capacity):
@@ -112,92 +135,71 @@
     slots = group * capacity
     cells = HB * EDGE * EDGE
 
-    def kernel(ids_ref, owner_ref, near_ref, latents_ref, out_ref, ids_out, entry_of, used_by,
-               flags, win, pick, sem):
+    def kernel(ids_ref, owner_ref, near_ref, latents_ref, out_ref, flags, win, pick, sem):
         me = lax.axis_index("grp")
-        for slot in range(slots):
-            entry_of[slot] = -1
-        for owner in range(group):
-            used_by[owner] = 0
-        for entry in range(listed):
-            owner = jnp.clip(owner_ref[entry], 0, group - 1)
-            rank = used_by[owner]
-
-            @pl.when((ids_ref[entry] >= 0) & (rank < capacity))
-            def _():
-                entry_of[owner * capacity + rank] = entry
-                used_by[owner] = rank + 1
-
-        entries = [entry_of[slot] for slot in range(slots)]
-        bricks = [
-            jnp.where(entry >= 0, ids_ref[jnp.maximum(entry, 0)], -1) for entry in entries
-        ]
-        finish = cut_windows(bricks, latents_ref, 0, HB, win, sem, pick, out_ref, 0)
-
-        lane = lax.broadcasted_iota(jnp.int32, (1, 128), 1)
-        told = jnp.full((1, 128), -1, jnp.int32)
-        for slot in range(slots):
-            told = jnp.where(lane == slot, bricks[slot], told)
-        for owner in range(group):
-            ids_out[owner] = told
-
+        bricks = [ids_ref[entry] for entry in range(listed)]
+        owners = [owner_ref[entry] for entry in range(listed)]
+        target, cell, finish = cut_windows(
+            bricks, owners, latents_ref, 0, HB, win, sem, pick, out_ref, 0
+        )
         offset = lax.broadcasted_iota(jnp.int32, (1, 27), 1)
         step_x = offset // 9 - 1
         step_y = offset // 3 % 3 - 1
         step_z = offset % 3 - 1
         inside_x = (me + step_x >= 0) & (me + step_x < group)
         flags[...] = jnp.zeros_like(flags)
-        for slot in range(slots):
-            safe = jnp.maximum(bricks[slot], 0)
-            near_y = lax.rem(lax.div(safe, across), across) + step_y
-            near_z = lax.rem(safe, across) + step_z
+        for entry in range(listed):
+            along_y, along_z = brick_place(bricks[entry], across)
+            near_y = along_y + step_y
+            near_z = along_z + step_z
             inside = inside_x & (near_y >= 0) & (near_y < across)
             inside = inside & (near_z >= 0) & (near_z < across)
-            near = near_ref[pl.ds(jnp.maximum(entries[slot], 0), 1), :]
-            chosen = (near > 0) | (offset == 13)
-            used = jnp.where(bricks[slot] >= 0, 1.0, 0.0)
-            flags[slot : slot + 1, 0:27] = jnp.where(inside & chosen, used, 0.0)
-        out_ref[:, cells] = flags[...].astype(jnp.bfloat16).reshape(group, capacity, channels)
+            chosen = (near_ref[entry : entry + 1, :] > 0) | (offset == 13)
+            flags[entry * WIN : entry * WIN + 1, 0:27] = jnp.where(inside & chosen, 1.0, 0.0)
+        at = lax.broadcasted_iota(jnp.int32, (slots, listed * WIN), 0)
+        chosen = jnp.where((at == target) & (cell == 0), 1.0, 0.0).astype(jnp.bfloat16)
+        slot_flags = jnp.dot(
+            chosen, flags[...].astype(jnp.bfloat16), preferred_element_type=jnp.float32
+        )
+        out_ref[:, cells] = slot_flags.astype(jnp.bfloat16).reshape(group, capacity, channels)
         finish()
 
     return pl.pallas_call(
         kernel,
         in_specs=[SMEM, SMEM, VMEM, HBM],
-        out_specs=[VMEM, VMEM],
-        out_shape=[
-            jax.ShapeDtypeStruct((group, cells + 1, capacity, channels), jnp.bfloat16),
-            jax.ShapeDtypeStruct((group, 1, 128), jnp.int32),
-        ],
+        out_specs=VMEM,
+        out_shape=jax.ShapeDtypeStruct((group, cells + 1, capacity, channels), jnp.bfloat16),
         scratch_shapes=[
-            pltpu.SMEM((slots,), jnp.int32),
-            pltpu.SMEM((group,), jnp.int32),
-            pltpu.VMEM((slots, 128), jnp.float32),
-            pltpu.VMEM((slots, HB, EDGE, WIN, channels), jnp.bfloat16),
-            pltpu.VMEM((2, EDGE * slots, slots * WIN), jnp.bfloat16),
-            pltpu.SemaphoreType.DMA((slots,)),
+            pltpu.VMEM((listed * WIN, channels), jnp.float32),
+            pltpu.VMEM((listed, HB, EDGE, WIN, channels), jnp.bfloat16),
+            pltpu.VMEM((2, EDGE * slots, listed * WIN), jnp.bfloat16),
+            pltpu.SemaphoreType.DMA((listed,)),
         ],
         compiler_params=pltpu.CompilerParams(vmem_limit_bytes=BIG),
         cost_estimate=cost(1_000_000_000, 3_000_000),
     )(brick_ids, brick_owner, neighbor_live, latents)
 
 
-def gather_rims(latents, heard, group, capacity):
+def gather_rims(latents, heard, listed, group, capacity):
     channels = latents.shape[3]
     slots = group * capacity
     plane_cells = EDGE * EDGE
 
     def kernel(heard_ref, latents_ref, out_ref, win_b, win_a, pick_b, pick_a, sem):
         me = lax.axis_index("grp")
-        before = lax.rem(me + group - 1, group)
-        after = lax.rem(me + 1, group)
-        below = [jnp.where(me > 0, heard_ref[before, 0, slot], -1) for slot in range(slots)]
-        above = [
-            jnp.where(me < group - 1, heard_ref[after, 0, slot], -1) for slot in range(slots)
-        ]
-        finish_b = cut_windows(below, latents_ref, 0, 2, win_b, sem.at[0], pick_b, out_ref, 0)
+
+        def lists_of(device, near):
+            bricks = [
+                jnp.where(near, heard_ref[device, 0, entry], -1) for entry in range(listed)
+            ]
+            return bricks, [heard_ref[device, 0, listed + entry] for entry in range(listed)]
+
+        before = lists_of(jnp.where(me > 0, me - 1, group - 1), me > 0)
+        after = lists_of(jnp.where(me < group - 1, me + 1, 0), me < group - 1)
+        finish_b = cut_windows(*before, latents_ref, 0, 2, win_b, sem.at[0], pick_b, out_ref, 0)[2]
         finish_a = cut_windows(
-            above, latents_ref, HB - 1, 1, win_a, sem.at[1], pick_a, out_ref, 2 * plane_cells
-        )
+            *after, latents_ref, HB - 1, 1, win_a, sem.at[1], pick_a, out_ref, 2 * plane_cells
+        )[2]
         finish_b()
         finish_a()
 
@@ -209,30 +211,36 @@
             (group, 3 * plane_cells, capacity, channels), jnp.bfloat16
         ),
         scratch_shapes=[
-            pltpu.VMEM((slots, 2, EDGE, WIN, channels), jnp.bfloat16),
-            pltpu.VMEM((slots, 1, EDGE, WIN, channels), jnp.bfloat16),
-            pltpu.VMEM((2, EDGE * slots, slots * WIN), jnp.bfloat16),
-            pltpu.VMEM((2, EDGE * slots, slots * WIN), jnp.bfloat16),
-            pltpu.SemaphoreType.DMA((2, slots)),
+            pltpu.VMEM((listed, 2, EDGE, WIN, channels), jnp.bfloat16),
+            pltpu.VMEM((listed, 1, EDGE, WIN, channels), jnp.bfloat16),
+            pltpu.VMEM((2, EDGE * slots, listed * WIN), jnp.bfloat16),
+            pltpu.VMEM((2, EDGE * slots, listed * WIN), jnp.bfloat16),
+            pltpu.SemaphoreType.DMA((2, listed)),
         ],
         compiler_params=pltpu.CompilerParams(vmem_limit_bytes=BIG),
         cost_estimate=cost(1_000_000_000, 3_000_000),
     )(heard, latents)
 
 
+def weight_moves(parts_of, packed, sem, inward):
+    moves = []
+    start = 0
+    for i, part in enumerate(parts_of):
+        rows = packed.at[pl.ds(start, part.shape[0])]
+        source, target = (rows, part) if inward else (part, rows)
+        moves.append(pltpu.make_async_copy(source, target, sem.at[i]))
+        start += part.shape[0]
+    return moves
+
+
 def pair_weights(up_weight, first_weight, second_weight, after):
     c1, c2 = up_weight.shape[3:]
     quad = 4 * c2
     lookup = {(parity, shift): tap for parity in (0, 1) for tap, shift in taps[parity]}
 
-    def kernel(up_ref, first_ref, second_ref, after_ref, up_hbm, first_hbm, second_hbm,
-               up_out, first_out, second_out, sem):
-        moves = [
-            pltpu.make_async_copy(source, target, sem.at[i])
-            for i, (source, target) in enumerate(
-                ((up_out, up_hbm), (first_out, first_hbm), (second_out, second_hbm))
-            )
-        ]
+    def kernel(up_ref, first_ref, second_ref, after_ref, packed, up_out, first_out, second_out,
+               sem):
+        moves = weight_moves((up_out, first_out, second_out), packed, sem, False)
         for kx in range(3):
             for dy in (0, 1):
                 for dz in (0, 1):
@@ -242,13 +250,13 @@
                             ty = lookup.get((py, dy))
                             tz = lookup.get((pz, dz))
                             both.append(
-                                jnp.zeros((c1, c2), jnp.bfloat16)
+                                jnp.zeros((c2, c1), jnp.bfloat16)
                                 if ty is None or tz is None
                                 else up_ref[kx, ty, tz]
                             )
                         at = (dy * 2 + dz) * c1
-                        up_out[kx, at : at + c1, py * 2 * c2 : (py + 1) * 2 * c2] = (
-                            jnp.concatenate(both, axis=1)
+                        up_out[kx * 4 * c1 + at : kx * 4 * c1 + at + c1, py * 2 * c2 : (py + 1) * 2 * c2] = (
+                            jnp.concatenate(both, axis=0).T
                         )
         moves[0].start()
         for raw, out, move in (
@@ -282,17 +290,18 @@
         for move in moves:
             move.wait()
 
-    shapes = ((3, 4 * c1, quad), (12 * quad, quad), (12 * quad, quad))
+    shapes = ((12 * c1, quad), (12 * quad, quad), (12 * quad, quad))
+    assert sum(shape[0] for shape in shapes) <= WEIGHT_ROWS
     return pl.pallas_call(
         kernel,
         in_specs=[VMEM, VMEM, VMEM, HBM],
-        out_specs=[HBM] * 3,
-        out_shape=[jax.ShapeDtypeStruct(shape, jnp.bfloat16) for shape in shapes],
+        out_specs=HBM,
+        out_shape=jax.ShapeDtypeStruct((WEIGHT_ROWS, quad), jnp.bfloat16),
         scratch_shapes=[pltpu.VMEM(shape, jnp.bfloat16) for shape in shapes]
         + [pltpu.SemaphoreType.DMA((3,))],
         compiler_params=pltpu.CompilerParams(vmem_limit_bytes=BIG),
         cost_estimate=cost(1_000_000_000, 6_000_000),
-    )(up_weight, first_weight, second_weight, after)
+    )(jnp.swapaxes(up_weight, 3, 4), first_weight, second_weight, after)
 
 
 def pair_class(p):
@@ -316,21 +325,11 @@
             pltpu.VMEM((3, EP, EP, slots, quad // 2), jnp.bfloat16),
             pltpu.VMEM((3, HP, HP, slots, quad), jnp.bfloat16),
             pltpu.VMEM((slots, self.c1), jnp.float32),
-            pltpu.VMEM((3, 4 * self.c1, quad), jnp.bfloat16),
+            pltpu.VMEM((12 * self.c1, quad), jnp.bfloat16),
             pltpu.VMEM((12 * quad, quad), jnp.bfloat16),
             pltpu.VMEM((12 * quad, quad), jnp.bfloat16),
             pltpu.SemaphoreType.DMA((3,)),
         ]
-
-    @staticmethod
-    def fetch(sources, targets, sem):
-        moves = [
-            pltpu.make_async_copy(source, target, sem.at[i])
-            for i, (source, target) in enumerate(zip(sources, targets))
-        ]
-        for move in moves:
-            move.start()
-        return moves
 
     def masks(self, flags, emask, hmask, classes):
         half, c2 = self.quad // 2, self.quad // 4
@@ -373,12 +372,13 @@
         mask = jnp.concatenate([mask, mask], axis=1)
         shape = (EP, EP, self.slots, self.quad)
         near = self.patch(reg, px)
+        depth = 4 * self.c1
         if 0 in parities:
-            even = jnp.dot(near, up_ref[1], preferred_element_type=jnp.float32)
+            even = jnp.dot(near, up_ref[depth : 2 * depth], preferred_element_type=jnp.float32)
             ext[2 * px] = (even.astype(jnp.bfloat16) * mask).reshape(shape)
         if 1 in parities:
-            odd = jnp.dot(near, up_ref[2], preferred_element_type=jnp.float32)
-            odd += jnp.dot(self.patch(reg, px + 1), up_ref[0], preferred_element_type=jnp.float32)
+            odd = jnp.dot(near, up_ref[2 * depth : 3 * depth], preferred_element_type=jnp.float32)
+            odd += jnp.dot(self.patch(reg, px + 1), up_ref[0:depth], preferred_element_type=jnp.float32)
             ext[2 * px + 1] = (odd.astype(jnp.bfloat16) * mask).reshape(shape)
 
     def conv(self, source, x, pairs, weight_ref):
@@ -417,21 +417,22 @@
 INNER_H, INNER_O = (2, 7), (2, 5)
 KEPT_E = (2, 3, 7, 8)
 KEPT_H = (2, 3, 5, 6)
-
-
-def decode_inner(own, up_pairs, first_pairs, second_pairs):
+KEPT_ROWS = 64
+
+
+def decode_inner(own, pairs):
     group, _, capacity, c1 = own.shape
-    quad = up_pairs.shape[2]
+    quad = pairs.shape[1]
     slots = group * capacity
     plane = BE * BE * quad // 4
     steps = Decoder(slots, c1, quad)
     width = (INNER_O[1] - INNER_O[0]) * plane
 
-    def kernel(own_ref, up_in, first_in, second_in, out_ref, ext_out, hid_out,
+    def kernel(own_ref, packed, out_ref, kept,
                reg, ext, hid, emask, hmask, flags, up_ref, first_ref, second_ref, wsem, rows, sem):
-        weights = steps.fetch(
-            (up_in, first_in, second_in), (up_ref, first_ref, second_ref), wsem
-        )
+        weights = weight_moves((up_ref, first_ref, second_ref), packed, wsem, True)
+        for move in weights:
+            move.start()
         flags[...] = own_ref[:, HB * EDGE * EDGE].reshape(slots, c1).astype(jnp.float32)
 
         def load(y, carry):
@@ -451,7 +452,7 @@
         lax.fori_loop(1, HB, both, 0)
         steps.raise_cells(reg, up_ref, emask, ext, HB, (0,))
         copies = [
-            pltpu.make_async_copy(ext.at[e], ext_out.at[i], sem.at[i])
+            pltpu.make_async_copy(ext.at[e], kept.at[i], sem.at[i])
             for i, e in enumerate(KEPT_E)
         ]
         for copy in copies:
@@ -465,7 +466,9 @@
 
         lax.fori_loop(INNER_H[0], INNER_H[1], hide, 0)
         more = [
-            pltpu.make_async_copy(hid.at[h], hid_out.at[i], sem.at[4 + i])
+            pltpu.make_async_copy(
+                hid.at[h], kept.at[4 + i, pl.ds(0, HP), pl.ds(0, HP)], sem.at[4 + i]
+            )
             for i, h in enumerate(KEPT_H)
         ]
         for copy in more:
@@ -487,23 +490,22 @@
 
     return pl.pallas_call(
         kernel,
-        in_specs=[VMEM] + [HBM] * 3,
-        out_specs=[HBM] * 3,
+        in_specs=[VMEM, HBM],
+        out_specs=[HBM] * 2,
         out_shape=[
             jax.ShapeDtypeStruct((slots, BE * plane), jnp.bfloat16),
-            jax.ShapeDtypeStruct((len(KEPT_E), EP, EP, slots, quad), jnp.bfloat16),
-            jax.ShapeDtypeStruct((len(KEPT_H), HP, HP, slots, quad), jnp.bfloat16),
+            jax.ShapeDtypeStruct((KEPT_ROWS, EP, EP, slots, quad), jnp.bfloat16),
         ],
         scratch_shapes=steps.scratch()
         + [pltpu.VMEM((slots, width), jnp.bfloat16), pltpu.SemaphoreType.DMA((9,))],
-        compiler_params=pltpu.CompilerParams(vmem_limit_bytes=64_000_000),
+        compiler_params=pltpu.CompilerParams(vmem_limit_bytes=50_000_000),
         cost_estimate=cost(8_000_000_000, 6_000_000),
-    )(own, up_pairs, first_pairs, second_pairs)
-
-
-def decode_outer(own, rims, out, ext_kept, hid_kept, up_pairs, first_pairs, second_pairs):
+    )(own, pairs)
+
+
+def decode_outer(own, rims, out, kept, pairs):
     group, _, capacity, c1 = own.shape
-    quad = up_pairs.shape[2]
+    quad = pairs.shape[1]
     slots = group * capacity
     plane = BE * BE * quad // 4
     steps = Decoder(slots, c1, quad)
@@ -511,16 +513,18 @@
     low_o = INNER_O[0]
     high_o = BE - INNER_O[1]
 
-    def kernel(own_ref, rims_ref, up_in, first_in, second_in, ext_in, hid_in, out_in, out_ref,
+    def kernel(own_ref, rims_ref, packed, kept, out_in, out_ref,
                reg, ext, hid, emask, hmask, flags, up_ref, first_ref, second_ref, wsem, rows, sem):
-        weights = steps.fetch(
-            (up_in, first_in, second_in), (up_ref, first_ref, second_ref), wsem
-        )
+        weights = weight_moves((up_ref, first_ref, second_ref), packed, wsem, True)
+        for move in weights:
+            move.start()
         copies = [
-            pltpu.make_async_copy(ext_in.at[i], ext.at[e], sem.at[i])
+            pltpu.make_async_copy(kept.at[i], ext.at[e], sem.at[i])
             for i, e in enumerate(KEPT_E)
         ] + [
-            pltpu.make_async_copy(hid_in.at[i], hid.at[h], sem.at[4 + i])
+            pltpu.make_async_copy(
+                kept.at[4 + i, pl.ds(0, HP), pl.ds(0, HP)], hid.at[h], sem.at[4 + i]
+            )
             for i, h in enumerate(KEPT_H)
         ]
         for copy in copies:
@@ -590,7 +594,7 @@
 
     return pl.pallas_call(
         kernel,
-        in_specs=[VMEM] * 2 + [HBM] * 6,
+        in_specs=[VMEM] * 2 + [HBM] * 3,
         out_specs=HBM,
         out_shape=jax.ShapeDtypeStruct((slots, BE * plane), jnp.bfloat16),
         scratch_shapes=steps.scratch()
@@ -598,10 +602,10 @@
             pltpu.VMEM((slots, (low_o + high_o) * plane), jnp.bfloat16),
             pltpu.SemaphoreType.DMA((10,)),
         ],
-        input_output_aliases={7: 0},
-        compiler_params=pltpu.CompilerParams(vmem_limit_bytes=64_000_000),
+        input_output_aliases={4: 0},
+        compiler_params=pltpu.CompilerParams(vmem_limit_bytes=50_000_000),
         cost_estimate=cost(8_000_000_000, 6_000_000),
-    )(own, rims, up_pairs, first_pairs, second_pairs, ext_kept, hid_kept, out)
+    )(own, rims, pairs, kept, out)
 
 
 def to_owners(array):
@@ -610,18 +614,19 @@
 
 def local(latents, up_weight, first_weight, second_weight, brick_ids, brick_owner, neighbor_live):
     group = lax.axis_size("grp")
-    capacity = max(2, brick_ids.shape[0] // group)
+    listed = brick_ids.shape[0]
+    capacity = max(2, listed // group)
     assert latents.shape[0] == HB
-    own, told = gather_own(
-        latents, brick_ids, brick_owner, neighbor_live, group, capacity
-    )
+    shape = (group, 1, listed)
+    lists = [jnp.broadcast_to(each, shape) for each in (brick_ids, brick_owner)]
+    heard = to_owners(jnp.concatenate(lists, axis=2))
+    own = gather_own(latents, brick_ids, brick_owner, neighbor_live, group, capacity)
     own = to_owners(own)
-    heard = to_owners(told)
-    rims = gather_rims(latents, heard, group, capacity)
+    rims = gather_rims(latents, heard, listed, group, capacity)
     rims = to_owners(rims)
     pairs = pair_weights(up_weight, first_weight, second_weight, heard)
-    out, ext_kept, hid_kept = decode_inner(own, *pairs)
-    return decode_outer(own, rims, out, ext_kept, hid_kept, *pairs)
+    out, kept = decode_inner(own, pairs)
+    return decode_outer(own, rims, out, kept, pairs)
 
 
 def solution(mesh):

time: 60.3 us -> 53.5 us (0.89)
  blocking collectives: 9.9 us -> 0 us
  Pallas kernels: 40.4 us -> 34.3 us
  starting transfers between devices: 7.09 us -> 12.3 us
  waiting for transfers between devices: 0.19 us -> 4.93 us
  local copies, waits for them, and re-layouts: 2.06 us -> 0.59 us
  other arithmetic: 0 us -> 0.75 us
    all_to_all x1 -> x0, blocking collectives: 9.9 us -> none  [to_owners(): return lax.all_to_all(array, 'grp', split_axis=0, concat_axis=0, tiled=True)]
    all_to_all x2 -> x3, starting transfers between devices: 7.09 us -> 12.3 us  [to_owners(): return lax.all_to_all(array, 'grp', split_axis=0, concat_axis=0, tiled=True)]
    all_to_all x2 -> x3, waiting for transfers between devices: 0.19 us -> 4.93 us  [to_owners(): return lax.all_to_all(array, 'grp', split_axis=0, concat_axis=0, tiled=True)]
    pallas_call x4, Pallas kernels: 32.8 us -> 29 us  [the longest x1 11.3 us: decode_outer(): pl.pallas_call(kernel, in_specs=[VMEM] * 2 + [HBM] * 3, out_specs=HBM, ou...]
    pallas_call x1, Pallas kernels: 7.54 us -> 5.25 us  [gather_rims(): pl.pallas_call(kernel, in_specs=[SMEM, HBM], out_specs=VMEM, out_shape=ja...]
    unnamed x7 -> x2, local copies, waits for them, and re-layouts: 2.06 us -> 0.01 us
    concatenate x0 -> x1, other arithmetic: none -> 0.75 us  [local(): heard = to_owners(jnp.concatenate(lists, axis=2))]
  transfers between devices with their start and end apart: 2 -> 3, of which waited for: 1 -> 3; matrix products, arithmetic and copies ran while one was open for 2% -> 0% of each run, Pallas kernels for 38% -> 43%
where the time goes in v3:
time: 53.5 us; the launch traced here: 52.9 us
  Pallas kernels  34.3 us (64%)
  starting transfers between devices  12.3 us (23%)
  waiting for transfers between devices  4.93 us (9%)
  other arithmetic  0.75 us (1%)
  local copies, waits for them, and re-layouts  0.59 us (1%)
    all_to_all x3, starting transfers between devices, to_owners(): return lax.all_to_all(array, 'grp', split_axis=0, concat_axis=0, tiled=True)  12.3 us
    pallas_call x1, Pallas kernels, decode_outer(): pl.pallas_call(kernel, in_specs=[VMEM] * 2 + [HBM] * 3, out_specs=HBM, ou...  11.3 us
    pallas_call x1, Pallas kernels, decode_inner(): pl.pallas_call(kernel, in_specs=[VMEM, HBM], out_specs=[HBM] * 2, out_sha...  10.1 us
    pallas_call x1, Pallas kernels, gather_rims(): pl.pallas_call(kernel, in_specs=[SMEM, HBM], out_specs=VMEM, out_shape=ja...  5.25 us
    all_to_all x3, waiting for transfers between devices, to_owners(): return lax.all_to_all(array, 'grp', split_axis=0, concat_axis=0, tiled=True)  4.93 us
    pallas_call x1, Pallas kernels, gather_own(): pl.pallas_call(kernel, in_specs=[SMEM, SMEM, VMEM, HBM], out_specs=VMEM,...  4.08 us
    pallas_call x1, Pallas kernels, pair_weights(): pl.pallas_call(kernel, in_specs=[VMEM, VMEM, VMEM, HBM], out_specs=HBM, o...  3.59 us
  transfers between devices with their start and end apart: 3, of which 3 were waited for; matrix products, arithmetic and copies ran while one was open for 0% of the time, Pallas kernels for 43%

profile of v3, /device:TPU:0, one launch (start us, length us, event | category | flops | bytes accessed | tf_op | source)
XLA Modules:
  0.0 52.9 jit_solution(9452006656603058698)
XLA Ops:
  0.0 0.7 %pad_add_fusion = s32[32]{0:T(128)S(1)} fusion(s32[16]{0:T(128)} %owner_ref.1, s32[16]{0:T(128)} %ids_ref.1), kind=kLoop, calls=%fused_computation | loop fusion | flops 32 | bytes 256 | tf_op jit(solution)/shard_map/concatenate | solution.py:622
  0.7 0.6 %broadcast.2 = s32[8,1,32]{2,1,0:T(1,128)} broadcast(s32[32]{0:T(128)S(1)} %pad_add_fusion), dimensions={2} | broadcast | bytes 1152 | tf_op jit(solution)/shard_map/concatenate | solution.py:622
  1.3 5.2 %all-to-all-start.1 = ((s32[8,1,32]{2,1,0:T(1,128)}), s32[8,1,32]{2,1,0:T(1,128)S(1)}, u32[]{:S(2)}, u32[]{:S(2)}) async-start(s32[8,1,32]{2,1,0:T(1,128)} %broadcast.2), calls=%async_computation.1 | async-start | bytes 8192 | tf_op jit(solution)/shard_map/all_to_all | solution.py:612
  6.5 4.1 %shard_map.73 = bf16[8,197,2,128]{3,2,1,0:T(2,128)(2,1)} custom-call(s32[16]{0:T(128)} %ids_ref.1, s32[16]{0:T(128)} %owner_ref.1, s32[16,27]{1,0:T(8,128)} %near_ref.1, bf16[4,64,64,128]{3,2,1,0:T(8,128)(2,1)} %latents_ref.3), custom_call_target="tpu_custom_call" | custom-call | flops 1000000000 | bytes 3000000 | tf_op jit(solution)/shard_map/pallas_call | solution.py:167
  10.6 0.6 %all-to-all-done.1.heard_ref.after_ref = s32[8,1,32]{2,1,0:T(1,128)S(1)} async-done(((s32[8,1,32]{2,1,0:T(1,128)}), s32[8,1,32]{2,1,0:T(1,128)S(1)}, u32[]{:S(2)}, u32[]{:S(2)}) %all-to-all-start.1) | async-done | bytes 1056 | tf_op jit(solution)/shard_map/all_to_all | solution.py:612
  11.2 0.0 copy-start
  11.2 3.6 %all-to-all-start = ((bf16[8,197,2,128]{3,2,1,0:T(2,128)(2,1)}), bf16[8,197,2,128]{3,2,1,0:T(2,128)(2,1)S(1)}, u32[]{:S(2)}, u32[]{:S(2)}) async-start(bf16[8,197,2,128]{3,2,1,0:T(2,128)(2,1)} %shard_map.73), calls=%async_computation | async-start | bytes 1613824 | tf_op jit(solution)/shard_map/all_to_all | solution.py:612
  14.8 0.0 copy-done
  14.8 5.3 %shard_map.74 = bf16[8,147,2,128]{3,2,1,0:T(2,128)(2,1)} custom-call(s32[8,1,32]{2,1,0:T(1,128)} %copy-done, bf16[4,64,64,128]{3,2,1,0:T(8,128)(2,1)} %latents_ref.3), custom_call_target="tpu_custom_call" | custom-call | flops 1000000000 | bytes 3000000 | tf_op jit(solution)/shard_map/pallas_call | solution.py:206
  20.1 3.6 %shard_map.75.packed = bf16[36864,256]{1,0:T(8,128)(2,1)} custom-call(bf16[3,3,3,64,128]{4,3,2,1,0:T(8,128)(2,1)} %bitcast.1, bf16[3,3,3,64,64]{4,3,2,1,0:T(8,128)(2,1)} %first_ref.1, bf16[3,3,3,64,64]{4,3,2,1,0:T(8,128)(2,1)} %second_ref.1, s32[8,1,32]{2,1,0:T(1,128)} %copy-done), custom_call_target="tpu_custom_call" | custom-call | flops 1000000000 | bytes 6000000 | tf_op jit(solution)/shard_map/pallas_call | solution.py:295
  23.7 3.9 %all-to-all-done.own_ref = bf16[8,197,2,128]{3,2,1,0:T(2,128)(2,1)S(1)} async-done(((bf16[8,197,2,128]{3,2,1,0:T(2,128)(2,1)}), bf16[8,197,2,128]{3,2,1,0:T(2,128)(2,1)S(1)}, u32[]{:S(2)}, u32[]{:S(2)}) %all-to-all-start) | async-done | bytes 806944 | tf_op jit(solution)/shard_map/all_to_all | solution.py:612
  27.6 3.5 %all-to-all-start.2 = ((bf16[8,147,2,128]{3,2,1,0:T(2,128)(2,1)}), bf16[8,147,2,128]{3,2,1,0:T(2,128)(2,1)S(1)}, u32[]{:S(2)}, u32[]{:S(2)}) async-start(bf16[8,147,2,128]{3,2,1,0:T(2,128)(2,1)} %shard_map.74), calls=%async_computation.2 | async-start | bytes 1204224 | tf_op jit(solution)/shard_map/all_to_all | solution.py:612
  31.2 10.1 %shard_map.76 = (bf16[16,32768]{1,0:T(8,128)(2,1)}, bf16[64,6,6,16,256]{4,3,2,1,0:T(8,128)(2,1)}) custom-call(bf16[8,197,2,128]{3,2,1,0:T(2,128)(2,1)S(1)} %all-to-all-done.own_ref, bf16[36864,256]{1,0:T(8,128)(2,1)} %shard_map.75.packed), custom_call_target="tpu_custom_call" | custom-call | flops 8000000000 | bytes 6000000 | tf_op jit(solution)/shard_map/pallas_call | solution.py:491
  41.3 0.4 all-to-all-done.2.rims_ref
  41.7 11.3 %shard_map.77 = bf16[16,32768]{1,0:T(8,128)(2,1)} custom-call(bf16[8,197,2,128]{3,2,1,0:T(2,128)(2,1)S(1)} %all-to-all-done.own_ref, bf16[8,147,2,128]{3,2,1,0:T(2,128)(2,1)S(1)} %all-to-all-done.2.rims_ref, bf16[36864,256]{1,0:T(8,128)(2,1)} %shard_map.75.packed, ...), custom_call_target="tpu_custom_call", output_to_operand_aliasing={{}: (4, {})} | custom-call | flops 8000000000 | bytes 6000000 | tf_op jit(solution)/shard_map/pallas_call | solution.py:595
Async XLA Ops:
  1.3 9.9 %all-to-all-start.1 = ((s32[8,1,32]{2,1,0:T(1,128)}), s32[8,1,32]{2,1,0:T(1,128)S(1)}, u32[]{:S(2)}, u32[]{:S(2)}) async-start(s32[8,1,32]{2,1,0:T(1,128)} %broadcast.2), calls=%async_computation.1 | async-start | bytes 8192 | tf_op jit(solution)/shard_map/all_to_all | solution.py:612
  11.2 3.6 %copy-start = (s32[8,1,32]{2,1,0:T(1,128)}, s32[8,1,32]{2,1,0:T(1,128)S(1)}, u32[]{:S(2)}) copy-start(s32[8,1,32]{2,1,0:T(1,128)S(1)} %all-to-all-done.1.heard_ref.after_ref) | copy-start | bytes 3076
  11.2 16.4 %all-to-all-start = ((bf16[8,197,2,128]{3,2,1,0:T(2,128)(2,1)}), bf16[8,197,2,128]{3,2,1,0:T(2,128)(2,1)S(1)}, u32[]{:S(2)}, u32[]{:S(2)}) async-start(bf16[8,197,2,128]{3,2,1,0:T(2,128)(2,1)} %shard_map.73), calls=%async_computation | async-start | bytes 1613824 | tf_op jit(solution)/shard_map/all_to_all | solution.py:612
  27.6 14.0 %all-to-all-start.2 = ((bf16[8,147,2,128]{3,2,1,0:T(2,128)(2,1)}), bf16[8,147,2,128]{3,2,1,0:T(2,128)(2,1)S(1)}, u32[]{:S(2)}, u32[]{:S(2)}) async-start(bf16[8,147,2,128]{3,2,1,0:T(2,128)(2,1)} %shard_map.74), calls=%async_computation.2 | async-start | bytes 1204224 | tf_op jit(solution)/shard_map/all_to_all | solution.py:612

commit v4 on v3

--- a/solution.py
+++ b/solution.py
@@ -13,6 +13,8 @@
 FAR = -1000
 BIG = 65_536_000
 WEIGHT_ROWS = 36_864
+INNER_ROWS = (320, 512, 512)
+OUTER_ROWS = (320, 512, 400)
 
 EEDGE = BE + 4
 HEDGE = BE + 2
@@ -313,8 +315,8 @@
 
 
 class Decoder:
-    def __init__(self, slots, c1, quad):
-        self.slots, self.c1, self.quad = slots, c1, quad
+    def __init__(self, slots, c1, quad, limits):
+        self.slots, self.c1, self.quad, self.limits = slots, c1, quad, limits
 
     def scratch(self):
         slots, quad = self.slots, self.quad
@@ -356,34 +358,33 @@
                             )
                         hmask[cx, py, pz, :, ty * half : (ty + 1) * half] = mixed[key]
 
-    def patch(self, reg, x):
-        return jnp.concatenate(
-            [
-                reg[x, dy : dy + EP, dz : dz + EP].reshape(-1, self.c1)
-                for dy in (0, 1)
-                for dz in (0, 1)
-            ],
-            axis=1,
-        )
-
-    def raise_cells(self, reg, up_ref, emask, ext, px, parities):
-        cx = jnp.where(px == 0, 0, jnp.where(px == EP - 1, 2, 1))
-        mask = emask[cx].reshape(-1, self.quad // 2)
-        mask = jnp.concatenate([mask, mask], axis=1)
-        shape = (EP, EP, self.slots, self.quad)
-        near = self.patch(reg, px)
+    def raise_cells(self, reg, up_ref, emask, ext, edges):
         depth = 4 * self.c1
-        if 0 in parities:
-            even = jnp.dot(near, up_ref[depth : 2 * depth], preferred_element_type=jnp.float32)
-            ext[2 * px] = (even.astype(jnp.bfloat16) * mask).reshape(shape)
-        if 1 in parities:
-            odd = jnp.dot(near, up_ref[2 * depth : 3 * depth], preferred_element_type=jnp.float32)
-            odd += jnp.dot(self.patch(reg, px + 1), up_ref[0:depth], preferred_element_type=jnp.float32)
-            ext[2 * px + 1] = (odd.astype(jnp.bfloat16) * mask).reshape(shape)
-
-    def conv(self, source, x, pairs, weight_ref):
+        for parity, shifts in ((0, ((1, 0),)), (1, ((2, 0), (0, 1)))):
+            planes = [edge for edge in edges if edge % 2 == parity]
+            weight = jnp.concatenate(
+                [up_ref[tap * depth : (tap + 1) * depth] for tap, _ in shifts], axis=0
+            )
+            for blocks in self.chunks(planes, EP, 0):
+                pieces = [
+                    jnp.concatenate(
+                        [reg[x // 2 + shift, y + dy, z + dz] for x, y, z in blocks], axis=0
+                    )
+                    for _, shift in shifts
+                    for dy in (0, 1)
+                    for dz in (0, 1)
+                ]
+                value = jnp.dot(
+                    jnp.concatenate(pieces, axis=1), weight, preferred_element_type=jnp.float32
+                ).astype(jnp.bfloat16)
+                for i, (x, y, z) in enumerate(blocks):
+                    mask = emask[pair_class(x // 2), y, z]
+                    mask = jnp.concatenate([mask, mask], axis=1)
+                    ext[x, y, z] = value[i * self.slots : (i + 1) * self.slots] * mask
+
+    def conv(self, source, blocks, weight_ref):
         pieces = [
-            source[x + kx, dy : dy + pairs, dz : dz + pairs].reshape(-1, self.quad)
+            jnp.concatenate([source[x + kx, y + dy, z + dz] for x, y, z in blocks], axis=0)
             for kx in range(3)
             for dy in (0, 1)
             for dz in (0, 1)
@@ -392,29 +393,34 @@
             jnp.concatenate(pieces, axis=1), weight_ref[...], preferred_element_type=jnp.float32
         )
 
-    def hide(self, ext, first_ref, hmask, hid, x):
-        value = self.conv(ext, x, HP, first_ref)
-        cx = jnp.where(x == 0, 0, jnp.where(x == HEDGE - 1, 2, 1))
-        value = (value * (1.0 / (1.0 + jnp.exp(-value)))).astype(jnp.bfloat16)
-        value = value * hmask[cx].reshape(-1, self.quad)
-        hid[x] = value.reshape(HP, HP, self.slots, self.quad)
-
-    def refine(self, ext, hid, second_ref, rows, x, at):
+    def chunks(self, planes, pairs, step):
+        blocks = [(x, y, z) for x in planes for y in range(pairs) for z in range(pairs)]
+        count = -(-len(blocks) * self.slots // self.limits[step])
+        ends = [len(blocks) * i // count for i in range(count + 1)]
+        return [blocks[start:end] for start, end in zip(ends, ends[1:])]
+
+    def hide(self, ext, first_ref, hmask, hid, planes):
+        for blocks in self.chunks(planes, HP, 1):
+            value = self.conv(ext, blocks, first_ref)
+            value = (value * (1.0 / (1.0 + jnp.exp(-value)))).astype(jnp.bfloat16)
+            for i, (x, y, z) in enumerate(blocks):
+                one = value[i * self.slots : (i + 1) * self.slots]
+                hid[x, y, z] = one * hmask[cell_class(x), y, z]
+
+    def refine(self, ext, hid, second_ref, rows, planes):
         half = self.quad // 2
-        value = self.conv(hid, x, OP, second_ref)
-        centre = ext[x + 2, 1 : 1 + OP, 1 : 1 + OP].reshape(-1, self.quad)
-        value = (value + centre.astype(jnp.float32)).astype(jnp.bfloat16)
-        value = value.reshape(OP, OP, self.slots, self.quad)
-        for py in range(OP):
-            for ty in (0, 1):
-                line = jnp.concatenate(
-                    [value[py, pz, :, ty * half : (ty + 1) * half] for pz in range(OP)], axis=1
-                )
-                start = pl.multiple_of(at * BE * OP * half + (2 * py + ty) * OP * half, 128)
-                rows[:, pl.ds(start, OP * half)] = line
-
-
-INNER_H, INNER_O = (2, 7), (2, 5)
+        for blocks in self.chunks(planes, OP, 2):
+            value = self.conv(hid, blocks, second_ref)
+            for i, (x, y, z) in enumerate(blocks):
+                one = value[i * self.slots : (i + 1) * self.slots]
+                one = one + ext[x + 2, y + 1, z + 1].astype(jnp.float32)
+                one = one.astype(jnp.bfloat16)
+                for ty in (0, 1):
+                    line = (planes.index(x) * BE + 2 * y + ty) * OP + z
+                    rows[:, line * half : (line + 1) * half] = one[:, ty * half : (ty + 1) * half]
+
+
+INNER_E, INNER_H, INNER_O = (2, 9), (2, 7), (2, 5)
 KEPT_E = (2, 3, 7, 8)
 KEPT_H = (2, 3, 5, 6)
 KEPT_ROWS = 64
@@ -425,7 +431,7 @@
     quad = pairs.shape[1]
     slots = group * capacity
     plane = BE * BE * quad // 4
-    steps = Decoder(slots, c1, quad)
+    steps = Decoder(slots, c1, quad, INNER_ROWS)
     width = (INNER_O[1] - INNER_O[0]) * plane
 
     def kernel(own_ref, packed, out_ref, kept,
@@ -445,12 +451,7 @@
         steps.masks(flags, emask, hmask, (1,))
         weights[0].wait()
 
-        def both(px, carry):
-            steps.raise_cells(reg, up_ref, emask, ext, px, (0, 1))
-            return carry
-
-        lax.fori_loop(1, HB, both, 0)
-        steps.raise_cells(reg, up_ref, emask, ext, HB, (0,))
+        steps.raise_cells(reg, up_ref, emask, ext, list(range(*INNER_E)))
         copies = [
             pltpu.make_async_copy(ext.at[e], kept.at[i], sem.at[i])
             for i, e in enumerate(KEPT_E)
@@ -460,11 +461,7 @@
 
         weights[1].wait()
 
-        def hide(x, carry):
-            steps.hide(ext, first_ref, hmask, hid, x)
-            return carry
-
-        lax.fori_loop(INNER_H[0], INNER_H[1], hide, 0)
+        steps.hide(ext, first_ref, hmask, hid, list(range(*INNER_H)))
         more = [
             pltpu.make_async_copy(
                 hid.at[h], kept.at[4 + i, pl.ds(0, HP), pl.ds(0, HP)], sem.at[4 + i]
@@ -476,11 +473,7 @@
 
         weights[2].wait()
 
-        def refine(x, carry):
-            steps.refine(ext, hid, second_ref, rows, x, x - INNER_O[0])
-            return carry
-
-        lax.fori_loop(INNER_O[0], INNER_O[1], refine, 0)
+        steps.refine(ext, hid, second_ref, rows, list(range(*INNER_O)))
         last = pltpu.make_async_copy(
             rows, out_ref.at[:, pl.ds(INNER_O[0] * plane, width)], sem.at[8]
         )
@@ -508,7 +501,7 @@
     quad = pairs.shape[1]
     slots = group * capacity
     plane = BE * BE * quad // 4
-    steps = Decoder(slots, c1, quad)
+    steps = Decoder(slots, c1, quad, OUTER_ROWS)
     plane_cells = EDGE * EDGE
     low_o = INNER_O[0]
     high_o = BE - INNER_O[1]
@@ -550,32 +543,23 @@
         steps.masks(flags, emask, hmask, (0, 1, 2))
         weights[0].wait()
 
-        def both(i, carry):
-            steps.raise_cells(reg, up_ref, emask, ext, i * (EP - 1), (0, 1))
-            return carry
-
-        lax.fori_loop(0, 2, both, 0)
-        steps.raise_cells(reg, up_ref, emask, ext, HB, (1,))
+        steps.raise_cells(
+            reg, up_ref, emask, ext, list(range(INNER_E[0])) + list(range(INNER_E[1], EEDGE))
+        )
         for copy in copies:
             copy.wait()
 
         weights[1].wait()
 
-        def hide(i, carry):
-            x = jnp.where(i < INNER_H[0], i, i + INNER_H[1] - INNER_H[0])
-            steps.hide(ext, first_ref, hmask, hid, x)
-            return carry
-
-        lax.fori_loop(0, HEDGE - INNER_H[1] + INNER_H[0], hide, 0)
-
+        steps.hide(
+            ext, first_ref, hmask, hid,
+            list(range(INNER_H[0])) + list(range(INNER_H[1], HEDGE)),
+        )
         weights[2].wait()
 
-        def refine(i, carry):
-            x = jnp.where(i < low_o, i, i + INNER_O[1] - low_o)
-            steps.refine(ext, hid, second_ref, rows, x, i)
-            return carry
-
-        lax.fori_loop(0, low_o + high_o, refine, 0)
+        steps.refine(
+            ext, hid, second_ref, rows, list(range(low_o)) + list(range(INNER_O[1], BE))
+        )
         ends = [
             pltpu.make_async_copy(
                 rows.at[:, pl.ds(0, low_o * plane)], out_ref.at[:, pl.ds(0, low_o * plane)],

time: 53.5 us -> 52.1 us (0.974)
  Pallas kernels: 34.3 us -> 31.3 us
  waiting for transfers between devices: 4.93 us -> 6.17 us
    pallas_call x1, Pallas kernels: 11.3 us -> 9.68 us  [decode_outer(): pl.pallas_call(kernel, in_specs=[VMEM] * 2 + [HBM] * 3, out_specs=HBM, ou...]
    pallas_call x1, Pallas kernels: 10.1 us -> 8.65 us  [decode_inner(): pl.pallas_call(kernel, in_specs=[VMEM, HBM], out_specs=[HBM] * 2, out_sha...]
    all_to_all x3, waiting for transfers between devices: 4.93 us -> 6.17 us  [to_owners(): return lax.all_to_all(array, 'grp', split_axis=0, concat_axis=0, tiled=True)]
  transfers between devices with their start and end apart: 3 -> 3, of which waited for: 3 -> 3; matrix products, arithmetic and copies ran while one was open for 0% -> 0% of each run, Pallas kernels for 43% -> 42%
where the time goes in v4:
time: 52.1 us; the launch traced here: 51.5 us
  Pallas kernels  31.3 us (60%)
  starting transfers between devices  12.5 us (24%)
  waiting for transfers between devices  6.17 us (12%)
  other arithmetic  0.75 us (1%)
  local copies, waits for them, and re-layouts  0.59 us (1%)
    all_to_all x3, starting transfers between devices, to_owners(): return lax.all_to_all(array, 'grp', split_axis=0, concat_axis=0, tiled=True)  12.5 us
    pallas_call x1, Pallas kernels, decode_outer(): pl.pallas_call(kernel, in_specs=[VMEM] * 2 + [HBM] * 3, out_specs=HBM, ou...  9.68 us
    pallas_call x1, Pallas kernels, decode_inner(): pl.pallas_call(kernel, in_specs=[VMEM, HBM], out_specs=[HBM] * 2, out_sha...  8.65 us
    all_to_all x3, waiting for transfers between devices, to_owners(): return lax.all_to_all(array, 'grp', split_axis=0, concat_axis=0, tiled=True)  6.17 us
    pallas_call x1, Pallas kernels, gather_rims(): pl.pallas_call(kernel, in_specs=[SMEM, HBM], out_specs=VMEM, out_shape=ja...  5.25 us
    pallas_call x1, Pallas kernels, gather_own(): pl.pallas_call(kernel, in_specs=[SMEM, SMEM, VMEM, HBM], out_specs=VMEM,...  4.08 us
    pallas_call x1, Pallas kernels, pair_weights(): pl.pallas_call(kernel, in_specs=[VMEM, VMEM, VMEM, HBM], out_specs=HBM, o...  3.59 us
  transfers between devices with their start and end apart: 3, of which 3 were waited for; matrix products, arithmetic and copies ran while one was open for 0% of the time, Pallas kernels for 42%

profile of v4, /device:TPU:0, one launch (start us, length us, event | category | flops | bytes accessed | tf_op | source)
XLA Modules:
  0.0 51.5 jit_solution(5018258704132809497)
XLA Ops:
  0.0 0.7 %pad_add_fusion = s32[32]{0:T(128)S(1)} fusion(s32[16]{0:T(128)} %owner_ref.1, s32[16]{0:T(128)} %ids_ref.1), kind=kLoop, calls=%fused_computation | loop fusion | flops 32 | bytes 256 | tf_op jit(solution)/shard_map/concatenate | solution.py:606
  0.7 0.6 %broadcast.2 = s32[8,1,32]{2,1,0:T(1,128)} broadcast(s32[32]{0:T(128)S(1)} %pad_add_fusion), dimensions={2} | broadcast | bytes 1152 | tf_op jit(solution)/shard_map/concatenate | solution.py:606
  1.3 5.2 %all-to-all-start.1 = ((s32[8,1,32]{2,1,0:T(1,128)}), s32[8,1,32]{2,1,0:T(1,128)S(1)}, u32[]{:S(2)}, u32[]{:S(2)}) async-start(s32[8,1,32]{2,1,0:T(1,128)} %broadcast.2), calls=%async_computation.1 | async-start | bytes 8192 | tf_op jit(solution)/shard_map/all_to_all | solution.py:596
  6.5 4.1 %shard_map.73 = bf16[8,197,2,128]{3,2,1,0:T(2,128)(2,1)} custom-call(s32[16]{0:T(128)} %ids_ref.1, s32[16]{0:T(128)} %owner_ref.1, s32[16,27]{1,0:T(8,128)} %near_ref.1, bf16[4,64,64,128]{3,2,1,0:T(8,128)(2,1)} %latents_ref.3), custom_call_target="tpu_custom_call" | custom-call | flops 1000000000 | bytes 3000000 | tf_op jit(solution)/shard_map/pallas_call | solution.py:169
  10.6 0.6 %all-to-all-done.1.heard_ref.after_ref = s32[8,1,32]{2,1,0:T(1,128)S(1)} async-done(((s32[8,1,32]{2,1,0:T(1,128)}), s32[8,1,32]{2,1,0:T(1,128)S(1)}, u32[]{:S(2)}, u32[]{:S(2)}) %all-to-all-start.1) | async-done | bytes 1056 | tf_op jit(solution)/shard_map/all_to_all | solution.py:596
  11.2 0.0 copy-start
  11.2 3.6 %all-to-all-start = ((bf16[8,197,2,128]{3,2,1,0:T(2,128)(2,1)}), bf16[8,197,2,128]{3,2,1,0:T(2,128)(2,1)S(1)}, u32[]{:S(2)}, u32[]{:S(2)}) async-start(bf16[8,197,2,128]{3,2,1,0:T(2,128)(2,1)} %shard_map.73), calls=%async_computation | async-start | bytes 1613824 | tf_op jit(solution)/shard_map/all_to_all | solution.py:596
  14.8 0.0 copy-done
  14.9 5.3 %shard_map.74 = bf16[8,147,2,128]{3,2,1,0:T(2,128)(2,1)} custom-call(s32[8,1,32]{2,1,0:T(1,128)} %copy-done, bf16[4,64,64,128]{3,2,1,0:T(8,128)(2,1)} %latents_ref.3), custom_call_target="tpu_custom_call" | custom-call | flops 1000000000 | bytes 3000000 | tf_op jit(solution)/shard_map/pallas_call | solution.py:208
  20.1 3.6 %shard_map.75.packed = bf16[36864,256]{1,0:T(8,128)(2,1)} custom-call(bf16[3,3,3,64,128]{4,3,2,1,0:T(8,128)(2,1)} %bitcast.1, bf16[3,3,3,64,64]{4,3,2,1,0:T(8,128)(2,1)} %first_ref.1, bf16[3,3,3,64,64]{4,3,2,1,0:T(8,128)(2,1)} %second_ref.1, s32[8,1,32]{2,1,0:T(1,128)} %copy-done), custom_call_target="tpu_custom_call" | custom-call | flops 1000000000 | bytes 6000000 | tf_op jit(solution)/shard_map/pallas_call | solution.py:297
  23.7 3.9 %all-to-all-done.own_ref = bf16[8,197,2,128]{3,2,1,0:T(2,128)(2,1)S(1)} async-done(((bf16[8,197,2,128]{3,2,1,0:T(2,128)(2,1)}), bf16[8,197,2,128]{3,2,1,0:T(2,128)(2,1)S(1)}, u32[]{:S(2)}, u32[]{:S(2)}) %all-to-all-start) | async-done | bytes 806944 | tf_op jit(solution)/shard_map/all_to_all | solution.py:596
  27.6 3.7 %all-to-all-start.2 = ((bf16[8,147,2,128]{3,2,1,0:T(2,128)(2,1)}), bf16[8,147,2,128]{3,2,1,0:T(2,128)(2,1)S(1)}, u32[]{:S(2)}, u32[]{:S(2)}) async-start(bf16[8,147,2,128]{3,2,1,0:T(2,128)(2,1)} %shard_map.74), calls=%async_computation.2 | async-start | bytes 1204224 | tf_op jit(solution)/shard_map/all_to_all | solution.py:596
  31.4 8.7 %shard_map.76 = (bf16[16,32768]{1,0:T(8,128)(2,1)}, bf16[64,6,6,16,256]{4,3,2,1,0:T(8,128)(2,1)}) custom-call(bf16[8,197,2,128]{3,2,1,0:T(2,128)(2,1)S(1)} %all-to-all-done.own_ref, bf16[36864,256]{1,0:T(8,128)(2,1)} %shard_map.75.packed), custom_call_target="tpu_custom_call" | custom-call | flops 8000000000 | bytes 6000000 | tf_op jit(solution)/shard_map/pallas_call | solution.py:484
  40.0 1.6 %all-to-all-done.2.rims_ref = bf16[8,147,2,128]{3,2,1,0:T(2,128)(2,1)S(1)} async-done(((bf16[8,147,2,128]{3,2,1,0:T(2,128)(2,1)}), bf16[8,147,2,128]{3,2,1,0:T(2,128)(2,1)S(1)}, u32[]{:S(2)}, u32[]{:S(2)}) %all-to-all-start.2) | async-done | bytes 602144 | tf_op jit(solution)/shard_map/all_to_all | solution.py:596
  41.7 9.7 %shard_map.77 = bf16[16,32768]{1,0:T(8,128)(2,1)} custom-call(bf16[8,197,2,128]{3,2,1,0:T(2,128)(2,1)S(1)} %all-to-all-done.own_ref, bf16[8,147,2,128]{3,2,1,0:T(2,128)(2,1)S(1)} %all-to-all-done.2.rims_ref, bf16[36864,256]{1,0:T(8,128)(2,1)} %shard_map.75.packed, ...), custom_call_target="tpu_custom_call", output_to_operand_aliasing={{}: (4, {})} | custom-call | flops 8000000000 | bytes 6000000 | tf_op jit(solution)/shard_map/pallas_call | solution.py:579
Async XLA Ops:
  1.3 9.9 %all-to-all-start.1 = ((s32[8,1,32]{2,1,0:T(1,128)}), s32[8,1,32]{2,1,0:T(1,128)S(1)}, u32[]{:S(2)}, u32[]{:S(2)}) async-start(s32[8,1,32]{2,1,0:T(1,128)} %broadcast.2), calls=%async_computation.1 | async-start | bytes 8192 | tf_op jit(solution)/shard_map/all_to_all | solution.py:596
  11.2 3.6 %copy-start = (s32[8,1,32]{2,1,0:T(1,128)}, s32[8,1,32]{2,1,0:T(1,128)S(1)}, u32[]{:S(2)}) copy-start(s32[8,1,32]{2,1,0:T(1,128)S(1)} %all-to-all-done.1.heard_ref.after_ref) | copy-start | bytes 3076
  11.2 16.4 %all-to-all-start = ((bf16[8,197,2,128]{3,2,1,0:T(2,128)(2,1)}), bf16[8,197,2,128]{3,2,1,0:T(2,128)(2,1)S(1)}, u32[]{:S(2)}, u32[]{:S(2)}) async-start(bf16[8,197,2,128]{3,2,1,0:T(2,128)(2,1)} %shard_map.73), calls=%async_computation | async-start | bytes 1613824 | tf_op jit(solution)/shard_map/all_to_all | solution.py:596
  27.6 14.0 %all-to-all-start.2 = ((bf16[8,147,2,128]{3,2,1,0:T(2,128)(2,1)}), bf16[8,147,2,128]{3,2,1,0:T(2,128)(2,1)S(1)}, u32[]{:S(2)}, u32[]{:S(2)}) async-start(bf16[8,147,2,128]{3,2,1,0:T(2,128)(2,1)} %shard_map.74), calls=%async_computation.2 | async-start | bytes 1204224 | tf_op jit(solution)/shard_map/all_to_all | solution.py:596

commit v5 on v4

--- a/solution.py
+++ b/solution.py
@@ -11,6 +11,7 @@
 EDGE = HB + 3
 WIN = 16
 FAR = -1000
+HALF = 65_536
 BIG = 65_536_000
 WEIGHT_ROWS = 36_864
 INNER_ROWS = (320, 512, 512)
@@ -191,10 +192,11 @@
         me = lax.axis_index("grp")
 
         def lists_of(device, near):
-            bricks = [
-                jnp.where(near, heard_ref[device, 0, entry], -1) for entry in range(listed)
-            ]
-            return bricks, [heard_ref[device, 0, listed + entry] for entry in range(listed)]
+            both = [heard_ref[device, 0, entry] for entry in range(listed)]
+            used = [near & (code >= 0) for code in both]
+            halves = [parts(jnp.maximum(code, 0), HALF) for code in both]
+            bricks = [jnp.where(use, half[0], -1) for use, half in zip(used, halves)]
+            return bricks, [half[1] for half in halves]
 
         before = lists_of(jnp.where(me > 0, me - 1, group - 1), me > 0)
         after = lists_of(jnp.where(me < group - 1, me + 1, 0), me < group - 1)
@@ -447,7 +449,7 @@
                     reg[1 + x, y, z] = own_ref[:, (x * EDGE + y) * EDGE + z].reshape(slots, c1)
             return carry
 
-        lax.fori_loop(0, EDGE, load, 0)
+        lax.fori_loop(0, EDGE, load, 0, unroll=True)
         steps.masks(flags, emask, hmask, (1,))
         weights[0].wait()
 
@@ -539,7 +541,7 @@
                 reg[HB + 2, y, z] = turned(plane_cells + at, 1)
             return carry
 
-        lax.fori_loop(0, EDGE, load, 0)
+        lax.fori_loop(0, EDGE, load, 0, unroll=True)
         steps.masks(flags, emask, hmask, (0, 1, 2))
         weights[0].wait()
 
@@ -601,9 +603,8 @@
     listed = brick_ids.shape[0]
     capacity = max(2, listed // group)
     assert latents.shape[0] == HB
-    shape = (group, 1, listed)
-    lists = [jnp.broadcast_to(each, shape) for each in (brick_ids, brick_owner)]
-    heard = to_owners(jnp.concatenate(lists, axis=2))
+    both = jnp.where(brick_ids >= 0, brick_ids * HALF + brick_owner, -1)
+    heard = to_owners(jnp.broadcast_to(both, (group, 1, listed)))
     own = gather_own(latents, brick_ids, brick_owner, neighbor_live, group, capacity)
     own = to_owners(own)
     rims = gather_rims(latents, heard, listed, group, capacity)

time: 52.1 us -> 52 us (level)
    concatenate x1 -> x0, other arithmetic: 0.75 us -> none  [local(): heard = to_owners(jnp.concatenate(lists, axis=2))]
    select_n x0 -> x1, other arithmetic: none -> 0.68 us  [local(): both = jnp.where(brick_ids >= 0, brick_ids * HALF + brick_owner, -1)]
    broadcast_in_dim x0 -> x1, local copies, waits for them, and re-layouts: none -> 0.59 us  [local(): heard = to_owners(jnp.broadcast_to(both, (group, 1, listed)))]
    concatenate x1 -> x0, local copies, waits for them, and re-layouts: 0.59 us -> none  [local(): heard = to_owners(jnp.concatenate(lists, axis=2))]
where the time goes in v5:
time: 52 us; the launch traced here: 51.4 us
  Pallas kernels  31.2 us (60%)
  starting transfers between devices  12.5 us (24%)
  waiting for transfers between devices  6.2 us (12%)
  other arithmetic  0.68 us (1%)
  local copies, waits for them, and re-layouts  0.59 us (1%)
    all_to_all x3, starting transfers between devices, to_owners(): return lax.all_to_all(array, 'grp', split_axis=0, concat_axis=0, tiled=True)  12.5 us
    pallas_call x1, Pallas kernels, decode_outer(): pl.pallas_call(kernel, in_specs=[VMEM] * 2 + [HBM] * 3, out_specs=HBM, ou...  9.68 us
    pallas_call x1, Pallas kernels, decode_inner(): pl.pallas_call(kernel, in_specs=[VMEM, HBM], out_specs=[HBM] * 2, out_sha...  8.65 us
    all_to_all x3, waiting for transfers between devices, to_owners(): return lax.all_to_all(array, 'grp', split_axis=0, concat_axis=0, tiled=True)  6.2 us
    pallas_call x1, Pallas kernels, gather_rims(): pl.pallas_call(kernel, in_specs=[SMEM, HBM], out_specs=VMEM, out_shape=ja...  5.22 us
    pallas_call x1, Pallas kernels, gather_own(): pl.pallas_call(kernel, in_specs=[SMEM, SMEM, VMEM, HBM], out_specs=VMEM,...  4.08 us
    pallas_call x1, Pallas kernels, pair_weights(): pl.pallas_call(kernel, in_specs=[VMEM, VMEM, VMEM, HBM], out_specs=HBM, o...  3.59 us
  transfers between devices with their start and end apart: 3, of which 3 were waited for; matrix products, arithmetic and copies ran while one was open for 0% of the time, Pallas kernels for 42%

profile of v5, /device:TPU:0, one launch (start us, length us, event | category | flops | bytes accessed | tf_op | source)
XLA Modules:
  0.0 51.4 jit_solution(8086724128710654487)
XLA Ops:
  0.0 0.7 %compare_select_fusion = s32[16]{0:T(128)S(1)} fusion(s32[16]{0:T(128)} %ids_ref.1, s32[16]{0:T(128)} %owner_ref.1), kind=kLoop, calls=%fused_computation | loop fusion | flops 64 | bytes 192 | tf_op jit(solution)/shard_map/jit(_where)/select_n | solution.py:606
  0.7 0.6 %broadcast_in_dim.8 = s32[8,1,16]{2,1,0:T(1,128)} broadcast(s32[16]{0:T(128)S(1)} %compare_select_fusion), dimensions={2} | broadcast | bytes 576 | tf_op jit(solution)/shard_map/broadcast_in_dim | solution.py:607
  1.3 5.2 %all-to-all-start.1 = ((s32[8,1,16]{2,1,0:T(1,128)}), s32[8,1,16]{2,1,0:T(1,128)S(1)}, u32[]{:S(2)}, u32[]{:S(2)}) async-start(s32[8,1,16]{2,1,0:T(1,128)} %broadcast_in_dim.8), calls=%async_computation.1 | async-start | bytes 8192 | tf_op jit(solution)/shard_map/all_to_all | solution.py:598
  6.5 4.1 %shard_map.73 = bf16[8,197,2,128]{3,2,1,0:T(2,128)(2,1)} custom-call(s32[16]{0:T(128)} %ids_ref.1, s32[16]{0:T(128)} %owner_ref.1, s32[16,27]{1,0:T(8,128)} %near_ref.1, bf16[4,64,64,128]{3,2,1,0:T(8,128)(2,1)} %latents_ref.3), custom_call_target="tpu_custom_call" | custom-call | flops 1000000000 | bytes 3000000 | tf_op jit(solution)/shard_map/pallas_call | solution.py:170
  10.6 0.6 %all-to-all-done.1.heard_ref.after_ref = s32[8,1,16]{2,1,0:T(1,128)S(1)} async-done(((s32[8,1,16]{2,1,0:T(1,128)}), s32[8,1,16]{2,1,0:T(1,128)S(1)}, u32[]{:S(2)}, u32[]{:S(2)}) %all-to-all-start.1) | async-done | bytes 544 | tf_op jit(solution)/shard_map/all_to_all | solution.py:598
  11.2 0.0 copy-start
  11.2 3.6 %all-to-all-start = ((bf16[8,197,2,128]{3,2,1,0:T(2,128)(2,1)}), bf16[8,197,2,128]{3,2,1,0:T(2,128)(2,1)S(1)}, u32[]{:S(2)}, u32[]{:S(2)}) async-start(bf16[8,197,2,128]{3,2,1,0:T(2,128)(2,1)} %shard_map.73), calls=%async_computation | async-start | bytes 1613824 | tf_op jit(solution)/shard_map/all_to_all | solution.py:598
  14.8 0.0 copy-done
  14.8 5.2 %shard_map.74 = bf16[8,147,2,128]{3,2,1,0:T(2,128)(2,1)} custom-call(s32[8,1,16]{2,1,0:T(1,128)} %copy-done, bf16[4,64,64,128]{3,2,1,0:T(8,128)(2,1)} %latents_ref.3), custom_call_target="tpu_custom_call" | custom-call | flops 1000000000 | bytes 3000000 | tf_op jit(solution)/shard_map/pallas_call | solution.py:210
  20.0 3.6 %shard_map.75.packed = bf16[36864,256]{1,0:T(8,128)(2,1)} custom-call(bf16[3,3,3,64,128]{4,3,2,1,0:T(8,128)(2,1)} %bitcast.1, bf16[3,3,3,64,64]{4,3,2,1,0:T(8,128)(2,1)} %first_ref.1, bf16[3,3,3,64,64]{4,3,2,1,0:T(8,128)(2,1)} %second_ref.1, s32[8,1,16]{2,1,0:T(1,128)} %copy-done), custom_call_target="tpu_custom_call" | custom-call | flops 1000000000 | bytes 6000000 | tf_op jit(solution)/shard_map/pallas_call | solution.py:299
  23.6 4.0 %all-to-all-done.own_ref = bf16[8,197,2,128]{3,2,1,0:T(2,128)(2,1)S(1)} async-done(((bf16[8,197,2,128]{3,2,1,0:T(2,128)(2,1)}), bf16[8,197,2,128]{3,2,1,0:T(2,128)(2,1)S(1)}, u32[]{:S(2)}, u32[]{:S(2)}) %all-to-all-start) | async-done | bytes 806944 | tf_op jit(solution)/shard_map/all_to_all | solution.py:598
  27.6 3.7 %all-to-all-start.2 = ((bf16[8,147,2,128]{3,2,1,0:T(2,128)(2,1)}), bf16[8,147,2,128]{3,2,1,0:T(2,128)(2,1)S(1)}, u32[]{:S(2)}, u32[]{:S(2)}) async-start(bf16[8,147,2,128]{3,2,1,0:T(2,128)(2,1)} %shard_map.74), calls=%async_computation.2 | async-start | bytes 1204224 | tf_op jit(solution)/shard_map/all_to_all | solution.py:598
  31.3 8.7 %shard_map.76 = (bf16[16,32768]{1,0:T(8,128)(2,1)}, bf16[64,6,6,16,256]{4,3,2,1,0:T(8,128)(2,1)}) custom-call(bf16[8,197,2,128]{3,2,1,0:T(2,128)(2,1)S(1)} %all-to-all-done.own_ref, bf16[36864,256]{1,0:T(8,128)(2,1)} %shard_map.75.packed), custom_call_target="tpu_custom_call" | custom-call | flops 8000000000 | bytes 6000000 | tf_op jit(solution)/shard_map/pallas_call | solution.py:486
  39.9 1.6 %all-to-all-done.2.rims_ref = bf16[8,147,2,128]{3,2,1,0:T(2,128)(2,1)S(1)} async-done(((bf16[8,147,2,128]{3,2,1,0:T(2,128)(2,1)}), bf16[8,147,2,128]{3,2,1,0:T(2,128)(2,1)S(1)}, u32[]{:S(2)}, u32[]{:S(2)}) %all-to-all-start.2) | async-done | bytes 602144 | tf_op jit(solution)/shard_map/all_to_all | solution.py:598
  41.6 9.7 %shard_map.77 = bf16[16,32768]{1,0:T(8,128)(2,1)} custom-call(bf16[8,197,2,128]{3,2,1,0:T(2,128)(2,1)S(1)} %all-to-all-done.own_ref, bf16[8,147,2,128]{3,2,1,0:T(2,128)(2,1)S(1)} %all-to-all-done.2.rims_ref, bf16[36864,256]{1,0:T(8,128)(2,1)} %shard_map.75.packed, ...), custom_call_target="tpu_custom_call", output_to_operand_aliasing={{}: (4, {})} | custom-call | flops 8000000000 | bytes 6000000 | tf_op jit(solution)/shard_map/pallas_call | solution.py:581
Async XLA Ops:
  1.3 9.9 %all-to-all-start.1 = ((s32[8,1,16]{2,1,0:T(1,128)}), s32[8,1,16]{2,1,0:T(1,128)S(1)}, u32[]{:S(2)}, u32[]{:S(2)}) async-start(s32[8,1,16]{2,1,0:T(1,128)} %broadcast_in_dim.8), calls=%async_computation.1 | async-start | bytes 8192 | tf_op jit(solution)/shard_map/all_to_all | solution.py:598
  11.2 3.6 %copy-start = (s32[8,1,16]{2,1,0:T(1,128)}, s32[8,1,16]{2,1,0:T(1,128)S(1)}, u32[]{:S(2)}) copy-start(s32[8,1,16]{2,1,0:T(1,128)S(1)} %all-to-all-done.1.heard_ref.after_ref) | copy-start | bytes 1540
  11.2 16.4 %all-to-all-start = ((bf16[8,197,2,128]{3,2,1,0:T(2,128)(2,1)}), bf16[8,197,2,128]{3,2,1,0:T(2,128)(2,1)S(1)}, u32[]{:S(2)}, u32[]{:S(2)}) async-start(bf16[8,197,2,128]{3,2,1,0:T(2,128)(2,1)} %shard_map.73), calls=%async_computation | async-start | bytes 1613824 | tf_op jit(solution)/shard_map/all_to_all | solution.py:598
  27.6 14.0 %all-to-all-start.2 = ((bf16[8,147,2,128]{3,2,1,0:T(2,128)(2,1)}), bf16[8,147,2,128]{3,2,1,0:T(2,128)(2,1)S(1)}, u32[]{:S(2)}, u32[]{:S(2)}) async-start(bf16[8,147,2,128]{3,2,1,0:T(2,128)(2,1)} %shard_map.74), calls=%async_computation.2 | async-start | bytes 1204224 | tf_op jit(solution)/shard_map/all_to_all | solution.py:598

commit v6 on v5

--- a/solution.py
+++ b/solution.py
@@ -71,7 +71,9 @@
     return jnp.where(owner_row >= 0, owner_row * capacity + rank, -1)
 
 
-def cut_windows(bricks, owners, latents_ref, plane, count, win, sem, pick, out_ref, base):
+def cut_windows(
+    bricks, owners, latents_ref, plane, count, win, sem, pick, out_ref, base, sent_ref, line_sem
+):
     grid = latents_ref.shape[1]
     channels = latents_ref.shape[3]
     listed = len(bricks)
@@ -107,6 +109,10 @@
         for copy in copies:
             copy.wait()
 
+        def leave(y):
+            some = pl.ds(base + y * count * EDGE, count * EDGE)
+            return pltpu.make_async_copy(out_ref.at[:, some], sent_ref.at[:, some], line_sem.at[y])
+
         def line(y, carry):
             rows = [jnp.clip(y + place[1], 0, EDGE - 1) for place in places]
             planes = [
@@ -114,18 +120,22 @@
                 for x in range(count)
             ]
             cut = jnp.dot(
-                pick[(y >= EDGE - 2).astype(jnp.int32)],
+                pick[int(y >= EDGE - 2)],
                 jnp.concatenate(planes, axis=1),
                 preferred_element_type=jnp.float32,
             ).astype(jnp.bfloat16)
             for x in range(count):
                 for z in range(EDGE):
-                    out_ref[:, base + (x * EDGE + y) * EDGE + z] = cut[
+                    out_ref[:, base + (y * count + x) * EDGE + z] = cut[
                         z * slots : (z + 1) * slots, x * channels : (x + 1) * channels
                     ].reshape(group, capacity, channels)
+            leave(y).start()
             return carry
 
-        lax.fori_loop(0, EDGE, line, 0, unroll=True)
+        for y in range(EDGE):
+            line(y, 0)
+        for y in range(EDGE):
+            leave(y).wait()
 
     return target, cell, finish
 
@@ -138,12 +148,13 @@
     slots = group * capacity
     cells = HB * EDGE * EDGE
 
-    def kernel(ids_ref, owner_ref, near_ref, latents_ref, out_ref, flags, win, pick, sem):
+    def kernel(ids_ref, owner_ref, near_ref, latents_ref, sent_ref, out_ref, flags, win, pick, sem,
+               line_sem):
         me = lax.axis_index("grp")
         bricks = [ids_ref[entry] for entry in range(listed)]
         owners = [owner_ref[entry] for entry in range(listed)]
         target, cell, finish = cut_windows(
-            bricks, owners, latents_ref, 0, HB, win, sem, pick, out_ref, 0
+            bricks, owners, latents_ref, 0, HB, win, sem, pick, out_ref, 0, sent_ref, line_sem
         )
         offset = lax.broadcasted_iota(jnp.int32, (1, 27), 1)
         step_x = offset // 9 - 1
@@ -165,18 +176,25 @@
             chosen, flags[...].astype(jnp.bfloat16), preferred_element_type=jnp.float32
         )
         out_ref[:, cells] = slot_flags.astype(jnp.bfloat16).reshape(group, capacity, channels)
+        last = pltpu.make_async_copy(
+            out_ref.at[:, pl.ds(cells, 1)], sent_ref.at[:, pl.ds(cells, 1)], line_sem.at[EDGE]
+        )
+        last.start()
         finish()
+        last.wait()
 
     return pl.pallas_call(
         kernel,
         in_specs=[SMEM, SMEM, VMEM, HBM],
-        out_specs=VMEM,
+        out_specs=HBM,
         out_shape=jax.ShapeDtypeStruct((group, cells + 1, capacity, channels), jnp.bfloat16),
         scratch_shapes=[
+            pltpu.VMEM((group, cells + 1, capacity, channels), jnp.bfloat16),
             pltpu.VMEM((listed * WIN, channels), jnp.float32),
             pltpu.VMEM((listed, HB, EDGE, WIN, channels), jnp.bfloat16),
             pltpu.VMEM((2, EDGE * slots, listed * WIN), jnp.bfloat16),
             pltpu.SemaphoreType.DMA((listed,)),
+            pltpu.SemaphoreType.DMA((EDGE + 1,)),
         ],
         compiler_params=pltpu.CompilerParams(vmem_limit_bytes=BIG),
         cost_estimate=cost(1_000_000_000, 3_000_000),
@@ -188,7 +206,8 @@
     slots = group * capacity
     plane_cells = EDGE * EDGE
 
-    def kernel(heard_ref, latents_ref, out_ref, win_b, win_a, pick_b, pick_a, sem):
+    def kernel(heard_ref, latents_ref, sent_ref, out_ref, win_b, win_a, pick_b, pick_a, sem,
+               line_sem):
         me = lax.axis_index("grp")
 
         def lists_of(device, near):
@@ -200,9 +219,13 @@
 
         before = lists_of(jnp.where(me > 0, me - 1, group - 1), me > 0)
         after = lists_of(jnp.where(me < group - 1, me + 1, 0), me < group - 1)
-        finish_b = cut_windows(*before, latents_ref, 0, 2, win_b, sem.at[0], pick_b, out_ref, 0)[2]
+        finish_b = cut_windows(
+            *before, latents_ref, 0, 2, win_b, sem.at[0], pick_b, out_ref, 0, sent_ref,
+            line_sem.at[0],
+        )[2]
         finish_a = cut_windows(
-            *after, latents_ref, HB - 1, 1, win_a, sem.at[1], pick_a, out_ref, 2 * plane_cells
+            *after, latents_ref, HB - 1, 1, win_a, sem.at[1], pick_a, out_ref, 2 * plane_cells,
+            sent_ref, line_sem.at[1],
         )[2]
         finish_b()
         finish_a()
@@ -210,16 +233,18 @@
     return pl.pallas_call(
         kernel,
         in_specs=[SMEM, HBM],
-        out_specs=VMEM,
+        out_specs=HBM,
         out_shape=jax.ShapeDtypeStruct(
             (group, 3 * plane_cells, capacity, channels), jnp.bfloat16
         ),
         scratch_shapes=[
+            pltpu.VMEM((group, 3 * plane_cells, capacity, channels), jnp.bfloat16),
             pltpu.VMEM((listed, 2, EDGE, WIN, channels), jnp.bfloat16),
             pltpu.VMEM((listed, 1, EDGE, WIN, channels), jnp.bfloat16),
             pltpu.VMEM((2, EDGE * slots, listed * WIN), jnp.bfloat16),
             pltpu.VMEM((2, EDGE * slots, listed * WIN), jnp.bfloat16),
             pltpu.SemaphoreType.DMA((2, listed)),
+            pltpu.SemaphoreType.DMA((2, EDGE)),
         ],
         compiler_params=pltpu.CompilerParams(vmem_limit_bytes=BIG),
         cost_estimate=cost(1_000_000_000, 3_000_000),
@@ -446,7 +471,7 @@
         def load(y, carry):
             for x in range(HB):
                 for z in range(EDGE):
-                    reg[1 + x, y, z] = own_ref[:, (x * EDGE + y) * EDGE + z].reshape(slots, c1)
+                    reg[1 + x, y, z] = own_ref[:, (y * HB + x) * EDGE + z].reshape(slots, c1)
             return carry
 
         lax.fori_loop(0, EDGE, load, 0, unroll=True)
@@ -535,10 +560,10 @@
             for z in range(EDGE):
                 at = y * EDGE + z
                 reg[0, y, z] = turned(2 * plane_cells + at, -1)
-                reg[1, y, z] = own_ref[:, at].reshape(slots, c1)
-                reg[HB, y, z] = own_ref[:, (HB - 1) * plane_cells + at].reshape(slots, c1)
-                reg[HB + 1, y, z] = turned(at, 1)
-                reg[HB + 2, y, z] = turned(plane_cells + at, 1)
+                reg[1, y, z] = own_ref[:, y * HB * EDGE + z].reshape(slots, c1)
+                reg[HB, y, z] = own_ref[:, (y * HB + HB - 1) * EDGE + z].reshape(slots, c1)
+                reg[HB + 1, y, z] = turned(2 * y * EDGE + z, 1)
+                reg[HB + 2, y, z] = turned((2 * y + 1) * EDGE + z, 1)
             return carry
 
         lax.fori_loop(0, EDGE, load, 0, unroll=True)

time: 52 us -> 51.9 us (level)
  waiting for transfers between devices: 6.2 us -> 5.62 us
    all_to_all x3, waiting for transfers between devices: 6.2 us -> 5.62 us  [to_owners(): return lax.all_to_all(array, 'grp', split_axis=0, concat_axis=0, tiled=True)]
  transfers between devices with their start and end apart: 3 -> 3, of which waited for: 3 -> 3; matrix products, arithmetic and copies ran while one was open for 0% -> 0% of each run, Pallas kernels for 42% -> 43%
where the time goes in v6:
time: 51.9 us; the launch traced here: 51.3 us
  Pallas kernels  31.7 us (61%)
  starting transfers between devices  12.5 us (24%)
  waiting for transfers between devices  5.62 us (11%)
  other arithmetic  0.68 us (1%)
  local copies, waits for them, and re-layouts  0.59 us (1%)
    all_to_all x3, starting transfers between devices, to_owners(): return lax.all_to_all(array, 'grp', split_axis=0, concat_axis=0, tiled=True)  12.5 us
    pallas_call x1, Pallas kernels, decode_outer(): pl.pallas_call(kernel, in_specs=[VMEM] * 2 + [HBM] * 3, out_specs=HBM, ou...  9.68 us
    pallas_call x1, Pallas kernels, decode_inner(): pl.pallas_call(kernel, in_specs=[VMEM, HBM], out_specs=[HBM] * 2, out_sha...  8.65 us
    pallas_call x1, Pallas kernels, gather_rims(): pl.pallas_call(kernel, in_specs=[SMEM, HBM], out_specs=HBM, out_shape=jax...  5.86 us
    all_to_all x3, waiting for transfers between devices, to_owners(): return lax.all_to_all(array, 'grp', split_axis=0, concat_axis=0, tiled=True)  5.62 us
    pallas_call x1, Pallas kernels, gather_own(): pl.pallas_call(kernel, in_specs=[SMEM, SMEM, VMEM, HBM], out_specs=HBM, o...  3.95 us
    pallas_call x1, Pallas kernels, pair_weights(): pl.pallas_call(kernel, in_specs=[VMEM, VMEM, VMEM, HBM], out_specs=HBM, o...  3.59 us
  transfers between devices with their start and end apart: 3, of which 3 were waited for; matrix products, arithmetic and copies ran while one was open for 0% of the time, Pallas kernels for 43%

profile of v6, /device:TPU:0, one launch (start us, length us, event | category | flops | bytes accessed | tf_op | source)
XLA Modules:
  0.0 51.3 jit_solution(16491007582638237649)
XLA Ops:
  0.0 0.7 %compare_select_fusion = s32[16]{0:T(128)S(1)} fusion(s32[16]{0:T(128)} %ids_ref.1, s32[16]{0:T(128)} %owner_ref.1), kind=kLoop, calls=%fused_computation | loop fusion | flops 64 | bytes 192 | tf_op jit(solution)/shard_map/jit(_where)/select_n | solution.py:631
  0.7 0.6 %broadcast_in_dim.8 = s32[8,1,16]{2,1,0:T(1,128)} broadcast(s32[16]{0:T(128)S(1)} %compare_select_fusion), dimensions={2} | broadcast | bytes 576 | tf_op jit(solution)/shard_map/broadcast_in_dim | solution.py:632
  1.3 5.2 %all-to-all-start.1 = ((s32[8,1,16]{2,1,0:T(1,128)}), s32[8,1,16]{2,1,0:T(1,128)S(1)}, u32[]{:S(2)}, u32[]{:S(2)}) async-start(s32[8,1,16]{2,1,0:T(1,128)} %broadcast_in_dim.8), calls=%async_computation.1 | async-start | bytes 8192 | tf_op jit(solution)/shard_map/all_to_all | solution.py:623
  6.5 4.0 %shard_map.73 = bf16[8,197,2,128]{3,2,1,0:T(2,128)(2,1)} custom-call(s32[16]{0:T(128)} %ids_ref.1, s32[16]{0:T(128)} %owner_ref.1, s32[16,27]{1,0:T(8,128)} %near_ref.1, bf16[4,64,64,128]{3,2,1,0:T(8,128)(2,1)} %latents_ref.3), custom_call_target="tpu_custom_call" | custom-call | flops 1000000000 | bytes 3000000 | tf_op jit(solution)/shard_map/pallas_call | solution.py:186
  10.4 0.7 %all-to-all-done.1.heard_ref.after_ref = s32[8,1,16]{2,1,0:T(1,128)S(1)} async-done(((s32[8,1,16]{2,1,0:T(1,128)}), s32[8,1,16]{2,1,0:T(1,128)S(1)}, u32[]{:S(2)}, u32[]{:S(2)}) %all-to-all-start.1) | async-done | bytes 544 | tf_op jit(solution)/shard_map/all_to_all | solution.py:623
  11.2 0.0 copy-start
  11.2 3.5 %all-to-all-start = ((bf16[8,197,2,128]{3,2,1,0:T(2,128)(2,1)}), bf16[8,197,2,128]{3,2,1,0:T(2,128)(2,1)S(1)}, u32[]{:S(2)}, u32[]{:S(2)}) async-start(bf16[8,197,2,128]{3,2,1,0:T(2,128)(2,1)} %shard_map.73), calls=%async_computation | async-start | bytes 1613824 | tf_op jit(solution)/shard_map/all_to_all | solution.py:623
  14.7 0.0 copy-done
  14.7 5.9 %shard_map.74 = bf16[8,147,2,128]{3,2,1,0:T(2,128)(2,1)} custom-call(s32[8,1,16]{2,1,0:T(1,128)} %copy-done, bf16[4,64,64,128]{3,2,1,0:T(8,128)(2,1)} %latents_ref.3), custom_call_target="tpu_custom_call" | custom-call | flops 1000000000 | bytes 3000000 | tf_op jit(solution)/shard_map/pallas_call | solution.py:233
  20.6 3.6 %shard_map.75.packed = bf16[36864,256]{1,0:T(8,128)(2,1)} custom-call(bf16[3,3,3,64,128]{4,3,2,1,0:T(8,128)(2,1)} %bitcast.1, bf16[3,3,3,64,64]{4,3,2,1,0:T(8,128)(2,1)} %first_ref.1, bf16[3,3,3,64,64]{4,3,2,1,0:T(8,128)(2,1)} %second_ref.1, s32[8,1,16]{2,1,0:T(1,128)} %copy-done), custom_call_target="tpu_custom_call" | custom-call | flops 1000000000 | bytes 6000000 | tf_op jit(solution)/shard_map/pallas_call | solution.py:324
  24.2 3.2 %all-to-all-done.own_ref = bf16[8,197,2,128]{3,2,1,0:T(2,128)(2,1)S(1)} async-done(((bf16[8,197,2,128]{3,2,1,0:T(2,128)(2,1)}), bf16[8,197,2,128]{3,2,1,0:T(2,128)(2,1)S(1)}, u32[]{:S(2)}, u32[]{:S(2)}) %all-to-all-start) | async-done | bytes 806944 | tf_op jit(solution)/shard_map/all_to_all | solution.py:623
  27.4 3.7 %all-to-all-start.2 = ((bf16[8,147,2,128]{3,2,1,0:T(2,128)(2,1)}), bf16[8,147,2,128]{3,2,1,0:T(2,128)(2,1)S(1)}, u32[]{:S(2)}, u32[]{:S(2)}) async-start(bf16[8,147,2,128]{3,2,1,0:T(2,128)(2,1)} %shard_map.74), calls=%async_computation.2 | async-start | bytes 1204224 | tf_op jit(solution)/shard_map/all_to_all | solution.py:623
  31.2 8.7 %shard_map.76 = (bf16[16,32768]{1,0:T(8,128)(2,1)}, bf16[64,6,6,16,256]{4,3,2,1,0:T(8,128)(2,1)}) custom-call(bf16[8,197,2,128]{3,2,1,0:T(2,128)(2,1)S(1)} %all-to-all-done.own_ref, bf16[36864,256]{1,0:T(8,128)(2,1)} %shard_map.75.packed), custom_call_target="tpu_custom_call" | custom-call | flops 8000000000 | bytes 6000000 | tf_op jit(solution)/shard_map/pallas_call | solution.py:511
  39.8 1.6 %all-to-all-done.2.rims_ref = bf16[8,147,2,128]{3,2,1,0:T(2,128)(2,1)S(1)} async-done(((bf16[8,147,2,128]{3,2,1,0:T(2,128)(2,1)}), bf16[8,147,2,128]{3,2,1,0:T(2,128)(2,1)S(1)}, u32[]{:S(2)}, u32[]{:S(2)}) %all-to-all-start.2) | async-done | bytes 602144 | tf_op jit(solution)/shard_map/all_to_all | solution.py:623
  41.5 9.7 %shard_map.77 = bf16[16,32768]{1,0:T(8,128)(2,1)} custom-call(bf16[8,197,2,128]{3,2,1,0:T(2,128)(2,1)S(1)} %all-to-all-done.own_ref, bf16[8,147,2,128]{3,2,1,0:T(2,128)(2,1)S(1)} %all-to-all-done.2.rims_ref, bf16[36864,256]{1,0:T(8,128)(2,1)} %shard_map.75.packed, ...), custom_call_target="tpu_custom_call", output_to_operand_aliasing={{}: (4, {})} | custom-call | flops 8000000000 | bytes 6000000 | tf_op jit(solution)/shard_map/pallas_call | solution.py:606
Async XLA Ops:
  1.3 9.9 %all-to-all-start.1 = ((s32[8,1,16]{2,1,0:T(1,128)}), s32[8,1,16]{2,1,0:T(1,128)S(1)}, u32[]{:S(2)}, u32[]{:S(2)}) async-start(s32[8,1,16]{2,1,0:T(1,128)} %broadcast_in_dim.8), calls=%async_computation.1 | async-start | bytes 8192 | tf_op jit(solution)/shard_map/all_to_all | solution.py:623
  11.2 3.6 %copy-start = (s32[8,1,16]{2,1,0:T(1,128)}, s32[8,1,16]{2,1,0:T(1,128)S(1)}, u32[]{:S(2)}) copy-start(s32[8,1,16]{2,1,0:T(1,128)S(1)} %all-to-all-done.1.heard_ref.after_ref) | copy-start | bytes 1540
  11.2 16.3 %all-to-all-start = ((bf16[8,197,2,128]{3,2,1,0:T(2,128)(2,1)}), bf16[8,197,2,128]{3,2,1,0:T(2,128)(2,1)S(1)}, u32[]{:S(2)}, u32[]{:S(2)}) async-start(bf16[8,197,2,128]{3,2,1,0:T(2,128)(2,1)} %shard_map.73), calls=%async_computation | async-start | bytes 1613824 | tf_op jit(solution)/shard_map/all_to_all | solution.py:623
  27.4 14.0 %all-to-all-start.2 = ((bf16[8,147,2,128]{3,2,1,0:T(2,128)(2,1)}), bf16[8,147,2,128]{3,2,1,0:T(2,128)(2,1)S(1)}, u32[]{:S(2)}, u32[]{:S(2)}) async-start(bf16[8,147,2,128]{3,2,1,0:T(2,128)(2,1)} %shard_map.74), calls=%async_computation.2 | async-start | bytes 1204224 | tf_op jit(solution)/shard_map/all_to_all | solution.py:623
